TPU v7x, 32 devices: a whole 2x2x4 slice. The times are simulated.
32 devices in a mesh: band: 8 (over y, x, core), cols: 4 (over z).
Axes of the slice: x: 2, y: 2, z: 4, core: 2. Of those that a mesh axis runs over, the one named last changes fastest.
Arguments:
- band_diagonals: float32 [256, 3072], P('cols', 'band'), may hold values from -0.4 to 0.4, as said below
- eigenvectors: float32 [3072, 512], P('band', 'cols'), may hold values from -4 to 4
Outputs:
- band_result: float32 [256, 3072], P('cols', 'band')
- transformed: float32 [3072, 512], P('band', 'cols')
Inputs may be any that keep to these rules, and one draw needn't show every extreme that they name: `band_diagonals`: entry [k, r] is the matrix's entry in row r and column r - k; it is zero where k > 128 or r < k.
All inputs are finite; a program needn't handle non-finite values.
Results may differ from a plain program's by a relative error of at most 0.0003.
Values sent between devices are 32-bit elements; how exact they have to be, the bound alone decides.
A program may use at most 64 MiB of HBM per device.

v0:
```python
import functools

import jax
import jax.numpy as jnp
from jax import lax
from jax.experimental import pallas as pl
from jax.experimental.pallas import tpu as pltpu
from jax.sharding import PartitionSpec as P

SWEEPS = 4
LAG = 3


def chase_kernel(blocks, half, blocks_dev, halo, piece_count, sweeps, *refs):
    band_ref, above_ref, eig_ref, under_ref, band_out, eig_out = refs[:6]
    refs = refs[2:]
    d_refs = refs[4 : 5 + sweeps]
    l_refs = refs[5 + sweeps : 6 + 2 * sweeps]
    v_refs = refs[6 + 2 * sweeps : 6 + 3 * sweeps]
    tau_refs = refs[6 + 3 * sweeps : 6 + 4 * sweeps]
    x_refs = refs[6 + 4 * sweeps : 6 + 5 * sweeps]
    edge_ref, rest_ref, turn_ref = refs[6 + 5 * sweeps :]
    steps = blocks - 2
    row = lax.broadcasted_iota(jnp.int32, (half, half), 0)
    col = lax.broadcasted_iota(jnp.int32, (half, half), 1)
    lane = lax.broadcasted_iota(jnp.int32, (1, half), 1)
    eye = row == col
    row8 = lax.broadcasted_iota(jnp.int32, (8, half), 0)
    col8 = lax.broadcasted_iota(jnp.int32, (8, half), 1)
    zero = jnp.zeros((half, half), jnp.float32)

    def slot(k):
        return jnp.clip(k, -1, blocks + 1) + 1

    def unpack(block):
        dev = block // blocks_dev
        part = block % blocks_dev
        start = pl.multiple_of(part * half, half)
        piece = band_ref[dev, :half, pl.ds(start, half)]
        extra = band_ref[dev, half : half + 1, pl.ds(start, half)]
        rows = pltpu.roll(piece.T, 1, 1, stride=1, stride_axis=0)
        d_refs[0][slot(block)] = jnp.where(row >= col, rows, rows.T)
        l_refs[0][slot(block - 1)] = jnp.where(
            col > row, rows, jnp.where(eye, jnp.broadcast_to(extra, (half, half)), 0.0)
        )

    def unpack_step(block, carry):
        unpack(block)
        return carry

    lax.fori_loop(0, blocks, unpack_step, 0)
    for extra_block in (blocks, blocks + 1):
        d_refs[0][extra_block + 1] = zero
    for extra_block in (blocks - 1, blocks, blocks + 1):
        l_refs[0][extra_block + 1] = zero
    edge_ref[...] = jnp.zeros(edge_ref.shape, jnp.float32)
    rest_ref[...] = zero

    def chain(s, t):
        k = t - LAG * s
        here, after, before = slot(k), slot(k + 1), slot(k - 1)
        old, new = s, s + 1
        d_prev, l_prev, d_now, l_now = d_refs[s], l_refs[s], d_refs[s + 1], l_refs[s + 1]
        active = (k >= 0) & (k < steps)
        limit = jnp.where(active, half, 0)
        pick = jnp.where(active, new, -1)
        x = x_refs[s][...]
        d_old, l_old, d_next = d_prev[here], l_prev[here], d_prev[after]
        l_next = l_prev[after, old : old + 1, :]
        left = l_now[before]

        lead = jnp.where(lane == old, d_next[old : old + 1, :], l_old[old : old + 1, :])
        lead_col = jnp.sum(
            jnp.where(eye, jnp.broadcast_to(lead, (half, half)), 0.0), axis=1, keepdims=True
        )
        window = jnp.where(row == old, lead, jnp.where(col == old, lead_col, d_old))
        rest_row = rest_ref[old : old + 1, :]
        feed = jnp.where(k == steps - 2, half, 0)
        corner = jnp.where(lane == old, l_next, jnp.where(lane < feed, rest_row, 0.0))
        if s > 0:
            rest_ref[...] = jnp.where(
                col == jnp.where(k == steps - 1, old, -1), l_old, rest_ref[...]
            )
        below = jnp.where(row == old, corner, jnp.where(col == old, d_next, l_old))

        rest = jnp.sum(jnp.where(row == new, 0.0, x * x), axis=0, keepdims=True)
        top = x[new : new + 1, :]
        length = jnp.sqrt(rest + top * top)
        v_top = top + length
        tau = 2.0 / (rest + v_top * v_top)
        tau = jnp.where(lane < limit, tau, 0.0)
        v_col = jnp.where(row < limit, jnp.where(row == new, v_top, x), 0.0)
        v_row = jnp.sum(jnp.where(eye, v_col, 0.0), axis=0, keepdims=True)

        beneath = jnp.sum(below * v_row, axis=1, keepdims=True)
        beneath = jnp.where(row < limit, beneath * tau, 0.0)
        first = k < 0
        source = jnp.where(first, old, new)
        head = jnp.where(row == old, l_next, d_next)
        early = jnp.where(first, half, 0)
        column = jnp.where(row < early, head, below)
        column = jnp.sum(jnp.where(col == source, column, 0.0), axis=1, keepdims=True)
        x_refs[s][...] = column - jnp.where(row < limit, beneath * v_top, 0.0)
        below = below - beneath * v_row

        inside = tau * jnp.sum(v_col * window, axis=0, keepdims=True)
        scale = 0.5 * tau * jnp.sum(v_row * inside, axis=1, keepdims=True)
        z_row = inside - scale * v_row
        z_col = jnp.sum(
            jnp.where(eye, jnp.broadcast_to(z_row, (half, half)), 0.0), axis=1, keepdims=True
        )
        window = window - v_col * z_row - z_col * v_row

        across = tau * jnp.sum(v_col * left, axis=0, keepdims=True)
        left = left - v_col * across
        left = jnp.where(col == pick, jnp.where(row == new, -length, 0.0), left)

        l_now[before] = left
        d_now[here] = window
        l_now[here] = below
        v_refs[s][here] = v_col
        tau_refs[s][here] = jnp.broadcast_to(tau, (8, half))

        start = jnp.where(k == 0, s, -1)
        edge = edge_ref[...]
        edge = jnp.where((row8 == start) & (col8 == s), d_old[:8], edge)
        below_start = jnp.where(k == 0, s + 1, -1)
        edge = jnp.where((row8 == below_start) & (col8 == s), -length, edge)
        edge_ref[...] = edge

    def wave(t, carry):
        for s in reversed(range(sweeps)):
            chain(s, t)
        return carry

    lax.fori_loop(-1, blocks + LAG * (sweeps - 1), wave, 0)

    device = lax.axis_index("band")
    base = device * blocks_dev - halo
    eig = [above_ref[e * half : (e + 1) * half, :] for e in range(halo)]
    eig += [eig_ref[e * half : (e + 1) * half, :] for e in range(blocks_dev)]
    eig.append(under_ref[...])
    for s in reversed(range(sweeps)):
        lead_rows = s + 1
        for e in range(sweeps - 1 - s + halo - sweeps, halo + blocks_dev):
            k = base + e
            v = v_refs[s][slot(k)]
            tau = tau_refs[s][slot(k), 0:1, :]
            low, high = eig[e], eig[e + 1]
            mixed = jnp.concatenate([jnp.where(row8 < lead_rows, high[:8], low[:8]), low[8:]], 0)
            inner = tau * jnp.sum(v * mixed, axis=0, keepdims=True)
            mixed = mixed - v * inner
            eig[e] = jnp.concatenate([jnp.where(row8 < lead_rows, low[:8], mixed[:8]), mixed[8:]], 0)
            top = jnp.where(row8 < lead_rows, mixed[:8], high[:8])
            eig[e + 1] = jnp.concatenate([top, high[8:]], 0) if high.shape[0] > 8 else top
    for m in range(blocks_dev):
        eig_out[m * half : (m + 1) * half, :] = eig[halo + m]

    d_last, l_last = d_refs[sweeps], l_refs[sweeps]
    edge = jnp.concatenate([edge_ref[...], zero[8:]], axis=0)
    rest = rest_ref[...]
    d_last[0] = jnp.where(row < sweeps, edge, 0.0)
    l_last[0] = jnp.where(row >= sweeps, edge, 0.0)
    flip = jnp.where((row + col == half) | ((row == 0) & (col == 0)), 1.0, 0.0)
    position = lax.axis_index("cols") * piece_count
    for m in range(blocks_dev):
        b = device * blocks_dev + m
        lim = jnp.where(b > 0, half, 0)
        rest_below = jnp.where(b == steps, half, 0)
        rest_last = jnp.where(b == steps + 1, half, 0)
        d_here, d_before = d_last[slot(b)], d_last[slot(b - 1)]
        l_here, l_before = l_last[slot(b - 1)], l_last[slot(b - 2)]
        c0 = jnp.where(
            row >= sweeps, jnp.where(col >= sweeps, d_here, l_here), jnp.where(col < sweeps, d_before, 0.0)
        )
        c1 = jnp.where(
            row >= sweeps,
            jnp.where(col >= sweeps, l_here, jnp.where(row < rest_below, rest, 0.0)),
            jnp.where(col >= sweeps, d_before, l_before),
        )
        c1 = jnp.where(row < lim, c1, 0.0)
        c2 = jnp.where(col >= sweeps, l_before, jnp.where(row < rest_last, rest, 0.0))
        c2 = jnp.where(row < sweeps, c2, 0.0)
        c2 = jnp.where(row < lim, c2, 0.0)
        lower = jnp.where(col <= row, c0, c1)
        upper = jnp.where(col <= row, c1, c2)
        for n, part in enumerate((lower, upper)):
            turned = jnp.dot(part, flip, precision=lax.Precision.HIGHEST)
            turned = pltpu.roll(turned, 0, 1, stride=1, stride_axis=0)
            turn_ref[n * half : (n + 1) * half, :] = turned.T
        band_out[:, m * half : (m + 1) * half] = turn_ref[pl.ds(pl.multiple_of(position, 8), piece_count), :]


def gather_kernel(half, devices, cols, takes, band_ref, eig_ref, all_ref, above_ref, under_ref, rev_ref, sems):
    z_send, z_recv, p_send, p_recv, c_send, c_recv, e_send, e_recv, own_sem = sems
    d, c = lax.axis_index("band"), lax.axis_index("cols")
    count = band_ref.shape[0]
    full = half // count
    pieces = full + 1
    chips = devices // 2
    tall = chips // 2
    chip, core = d // 2, d % 2
    partner = chip * 2 + 1 - core
    spot = (1 - chip % 2) * (chip // 2) + (chip % 2) * (chips - 1 - chip // 2)

    def at(rel):
        ring = (spot + rel + chips) % chips
        turn = ring // tall
        return ((1 - turn) * 2 * ring + turn * (2 * (chips - 1 - ring) + 1)) * 2 + core

    for r in range(count):
        rev_ref[r : r + 1, :] = band_ref[count - 1 - r : count - r, :]

    barrier = pltpu.get_barrier_semaphore()
    peers = [(at(1), c), (at(-1), c), (partner, c)]
    for hop in range(1, len(takes) + 1):
        peers += [((d + hop) % devices, c), ((d - hop + devices) % devices, c)]
    for peer in peers:
        pl.semaphore_signal(barrier, inc=1, device_id=peer, device_id_type=pl.DeviceIdType.MESH)

    @pl.when(c > 0)
    def _():
        pl.semaphore_signal(barrier, inc=1, device_id=(d, c - 1), device_id_type=pl.DeviceIdType.MESH)

    @pl.when(c < cols - 1)
    def _():
        pl.semaphore_signal(barrier, inc=1, device_id=(d, c + 1), device_id_type=pl.DeviceIdType.MESH)

    beside = (c + cols - 1) // cols + 1 - (c + 1) // cols
    pl.semaphore_wait(barrier, len(peers) + beside)

    def send(src, dst, send_sem, recv_sem, device):
        return pltpu.make_async_remote_copy(
            src_ref=src,
            dst_ref=dst,
            send_sem=send_sem,
            recv_sem=recv_sem,
            device_id=device,
            device_id_type=pl.DeviceIdType.MESH,
        )

    def rows_of(p, part):
        first, size = (half - (p + 1) * count, count) if p < full else (half, 8)
        if part is not None and p < full:
            first, size = first + part * (size // 2), size // 2
        return pl.ds(first, size)

    def place(dev, p, part=None):
        return all_ref.at[dev, rows_of(p, part)]

    def source(p):
        return rev_ref if p < full else band_ref.at[pl.ds(0, 8)]

    def along(p, up, src):
        to = (c + 1) % cols if up else (c - 1 + cols) % cols
        return send(src, place(d, p), z_send.at[p, int(up)], z_recv.at[p], (d, to))

    def hops(p):
        for j in range(1, chips // 2 + 1):
            for way in (1, -1):
                if 2 * j < chips:
                    yield j, way, None
                elif p < full:
                    yield j, way, 0 if way == 1 else 1
                elif way == 1:
                    yield j, way, None

    def across(p, j, way, part, src=None):
        dev = at(-way * (j - 1))
        src = place(dev, p, part) if src is None else src
        which = 2 * j + (way + 1) // 2
        return send(src, place(dev, p, part), p_send.at[p, which], p_recv.at[p, which], (at(way), c))

    def pair(p, j, way, part, src=None):
        dev = at(-way * j)
        src = place(dev, p, part) if src is None else src
        which = 2 * j + (way + 1) // 2
        return send(src, place(dev, p, part), c_send.at[p, which], c_recv.at[p, which], (partner, c))

    def own(p):
        return pltpu.make_async_copy(source(p), place(d, p), own_sem)

    def first_hops(p, src):
        for j, way, part in hops(p):
            if j == 1:
                across(p, 1, way, part, src).start()
        pair(p, 0, 1, None, src).start()

    rows_dev = eig_ref.shape[0]
    halos = []
    end = sum(takes)
    for hop, take in enumerate(takes, 1):
        halos.append(
            send(
                eig_ref.at[pl.ds(rows_dev - take, take)],
                above_ref.at[pl.ds(end - take, take)],
                e_send.at[hop],
                e_recv.at[hop],
                ((d + hop) % devices, c),
            )
        )
        end -= take
    halos.append(
        send(eig_ref.at[pl.ds(0, 8)], under_ref, e_send.at[0], e_recv.at[0], ((d - 1 + devices) % devices, c))
    )

    for p in range(pieces):

        @pl.when(c == p)
        def _():
            @pl.when(c < cols - 1)
            def _():
                along(p, True, source(p)).start()

            @pl.when(c > 0)
            def _():
                along(p, False, source(p)).start()

            first_hops(p, source(p))
            own(p).start()

    def receive(p):
        @pl.when(c != p)
        def _():
            along(p, True, place(d, p)).wait_recv()

            @pl.when((c > p) & (c < cols - 1))
            def _():
                along(p, True, place(d, p)).start()

            @pl.when((c < p) & (c > 0))
            def _():
                along(p, False, place(d, p)).start()

            first_hops(p, place(d, p))

    def relay(p, level):
        for j, way, part in hops(p):
            if j == level:
                across(p, j, way, part).wait_recv()
                for j2, way2, part2 in hops(p):
                    if j2 == j + 1 and way2 == way:
                        across(p, j2, way, part2).start()
                pair(p, j, way, part).start()

    for p in reversed(range(pieces)):
        receive(p)
    for halo in halos:
        halo.start()
    for level in range(1, chips // 2 + 1):
        for p in reversed(range(pieces)):
            relay(p, level)
    for p in range(pieces):

        @pl.when(c == p)
        def _():
            own(p).wait()

        @pl.when((c >= p) & (c < cols - 1))
        def _():
            along(p, True, place(d, p)).wait_send()

        @pl.when((c <= p) & (c > 0))
        def _():
            along(p, False, place(d, p)).wait_send()

        for j, way, part in hops(p):
            across(p, j, way, part).wait_send()
            pair(p, j, way, part).wait()
        pair(p, 0, 1, None).wait()
    for halo in halos:
        halo.wait()


def body(band_diagonals, eigenvectors):
    piece_count, rows_dev = band_diagonals.shape
    cols = lax.axis_size("cols")
    double = piece_count * cols
    half = double // 2
    blocks_dev = rows_dev // half
    devices = lax.axis_size("band")
    blocks = blocks_dev * devices
    sweeps = SWEEPS
    halo = sweeps
    columns = eigenvectors.shape[1]
    f32 = jnp.float32
    vmem = pl.BlockSpec(memory_space=pltpu.VMEM)

    takes = []
    while sum(takes) < halo * half:
        takes.append(min(halo * half - sum(takes), rows_dev))
    pieces = half // piece_count + 1
    dma = pltpu.SemaphoreType.DMA
    band, above, under = pl.pallas_call(
        functools.partial(gather_kernel, half, devices, cols, takes),
        out_shape=(
            jax.ShapeDtypeStruct((devices, half + 8, rows_dev), f32),
            jax.ShapeDtypeStruct((halo * half, columns), f32),
            jax.ShapeDtypeStruct((8, columns), f32),
        ),
        in_specs=[vmem] * 2,
        out_specs=(vmem,) * 3,
        scratch_shapes=[
            pltpu.VMEM((piece_count, rows_dev), f32),
            [
                dma((pieces, 2)),
                dma((pieces,)),
                dma((pieces, devices + 2)),
                dma((pieces, devices + 2)),
                dma((pieces, devices + 2)),
                dma((pieces, devices + 2)),
                dma((len(takes) + 1,)),
                dma((len(takes) + 1,)),
                dma,
            ]
        ],
        compiler_params=pltpu.CompilerParams(collective_id=0, has_side_effects=True),
    )(band_diagonals, eigenvectors)

    slots = blocks + 3
    scratch = (
        [pltpu.VMEM((slots, half, half), f32)] * (2 * (sweeps + 1))
        + [pltpu.VMEM((slots, half, half), f32)] * sweeps
        + [pltpu.VMEM((slots, 8, half), f32)] * sweeps
        + [pltpu.VMEM((half, half), f32)] * sweeps
        + [
            pltpu.VMEM((8, half), f32),
            pltpu.VMEM((half, half), f32),
            pltpu.VMEM((double, half), f32),
        ]
    )
    return pl.pallas_call(
        functools.partial(chase_kernel, blocks, half, blocks_dev, halo, piece_count, sweeps),
        out_shape=(
            jax.ShapeDtypeStruct((piece_count, rows_dev), f32),
            jax.ShapeDtypeStruct((rows_dev, columns), f32),
        ),
        in_specs=[vmem] * 4,
        out_specs=(vmem, vmem),
        scratch_shapes=scratch,
        compiler_params=pltpu.CompilerParams(vmem_limit_bytes=62 * 1024 * 1024),
    )(band, above, eigenvectors, under)


def solution(mesh):
    return jax.shard_map(
        body,
        mesh=mesh,
        in_specs=(P("cols", "band"), P("band", "cols")),
        out_specs=(P("cols", "band"), P("band", "cols")),
        check_vma=False,
    )
```

profile of v0, /device:TPU:25, one launch (start us, length us, event | category | flops | bytes accessed | tf_op | source)
XLA Modules:
  0.0 54.9 jit_solution(16473501939816969051)
XLA Ops:
  0.6 27.3 %shard_map.41 = (f32[8,136,384]{2,1,0:T(8,128)}, f32[512,128]{1,0:T(8,128)}, f32[8,128]{1,0:T(8,128)}) custom-call(f32[64,384]{1,0:T(8,128)} %band_ref.1, f32[384,128]{1,0:T(8,128)} %refs_2_.1), custom_call_target="tpu_custom_call" | custom-call | tf_op jit(solution)/shard_map/pallas_call | solution.py:394
  27.9 27.0 %shard_map.42 = (f32[64,384]{1,0:T(8,128)}, f32[384,128]{1,0:T(8,128)}) custom-call(f32[8,136,384]{2,1,0:T(8,128)} %get-tuple-element.5.refs_0_, f32[512,128]{1,0:T(8,128)} %get-tuple-element.6.refs_1_, f32[384,128]{1,0:T(8,128)} %refs_2_.1, f32[8,128]{1,0:T(8,128)} %get-tuple-element.7.refs_3_), custom_call_target="tpu_custom_call" | custom-call | tf_op jit(solution)/shard_map/pallas_call | solution.py:432
where the time goes:
time: 55 us; the launch traced here: 54.9 us
  Pallas kernels  54.2 us (99%)
  between operations  0.64 us (1%)
    pallas_call x1, Pallas kernels, body(): pl.pallas_call(functools.partial(gather_kernel, half, devices, cols, take...  27.3 us
    pallas_call x1, Pallas kernels, body(): pl.pallas_call(functools.partial(chase_kernel, blocks, half, blocks_dev,...  27 us

commit v1 on v0

--- a/solution.py
+++ b/solution.py
@@ -9,6 +9,7 @@
 
 SWEEPS = 4
 LAG = 3
+UNPACK = 2
 
 
 def chase_kernel(blocks, half, blocks_dev, halo, piece_count, sweeps, *refs):
@@ -18,8 +19,7 @@
     l_refs = refs[5 + sweeps : 6 + 2 * sweeps]
     v_refs = refs[6 + 2 * sweeps : 6 + 3 * sweeps]
     tau_refs = refs[6 + 3 * sweeps : 6 + 4 * sweeps]
-    x_refs = refs[6 + 4 * sweeps : 6 + 5 * sweeps]
-    edge_ref, rest_ref, turn_ref = refs[6 + 5 * sweeps :]
+    edge_ref, eye_ref, turn_ref = refs[6 + 4 * sweeps :]
     steps = blocks - 2
     row = lax.broadcasted_iota(jnp.int32, (half, half), 0)
     col = lax.broadcasted_iota(jnp.int32, (half, half), 1)
@@ -28,6 +28,7 @@
     row8 = lax.broadcasted_iota(jnp.int32, (8, half), 0)
     col8 = lax.broadcasted_iota(jnp.int32, (8, half), 1)
     zero = jnp.zeros((half, half), jnp.float32)
+    tiles = range(half // 8)
 
     def slot(k):
         return jnp.clip(k, -1, blocks + 1) + 1
@@ -39,8 +40,8 @@
         piece = band_ref[dev, :half, pl.ds(start, half)]
         extra = band_ref[dev, half : half + 1, pl.ds(start, half)]
         rows = pltpu.roll(piece.T, 1, 1, stride=1, stride_axis=0)
-        d_refs[0][slot(block)] = jnp.where(row >= col, rows, rows.T)
-        l_refs[0][slot(block - 1)] = jnp.where(
+        d_refs[0][block + 1] = jnp.where(row >= col, rows, rows.T)
+        l_refs[0][block] = jnp.where(
             col > row, rows, jnp.where(eye, jnp.broadcast_to(extra, (half, half)), 0.0)
         )
 
@@ -48,92 +49,115 @@
         unpack(block)
         return carry
 
-    lax.fori_loop(0, blocks, unpack_step, 0)
-    for extra_block in (blocks, blocks + 1):
-        d_refs[0][extra_block + 1] = zero
-    for extra_block in (blocks - 1, blocks, blocks + 1):
-        l_refs[0][extra_block + 1] = zero
+    lax.fori_loop(0, blocks, unpack_step, 0, unroll=UNPACK)
+    for level in range(sweeps):
+        d_refs[level][blocks + 1] = zero
+        l_refs[level][blocks + 1] = zero
+        v_refs[level][0] = zero
+        tau_refs[level][0] = zero[:8]
+    l_refs[0][blocks] = zero
+    eye_ref[...] = jnp.where(eye, 1.0, 0.0)
     edge_ref[...] = jnp.zeros(edge_ref.shape, jnp.float32)
-    rest_ref[...] = zero
-
-    def chain(s, t):
-        k = t - LAG * s
-        here, after, before = slot(k), slot(k + 1), slot(k - 1)
+
+    def load(ref, index):
+        return [ref[index, 8 * i : 8 * i + 8, :] for i in tiles]
+
+    def store(ref, index, parts):
+        for i in tiles:
+            ref[index, 8 * i : 8 * i + 8, :] = parts[i]
+
+    def tree(parts):
+        while len(parts) > 1:
+            parts = [a + b for a, b in zip(parts[::2], parts[1::2])]
+        return jnp.sum(parts[0], axis=0, keepdims=True)
+
+    def norms(x, new):
+        squares = [a * a for a in x]
+        squares[0] = jnp.where(row8 == new, 0.0, squares[0])
+        rest = tree(squares)
+        top = x[0][new : new + 1, :]
+        return rest, top, jnp.sqrt(rest + top * top)
+
+    def begin(s):
+        first = load(d_refs[s], 1)
+        corner = l_refs[s][1, s : s + 1, :]
+        first[0] = jnp.where(row8 == s, corner, first[0])
+        x = [jnp.broadcast_to(a[:, s : s + 1], (8, half)) for a in first]
+        store(v_refs[s], 1, x)
+        length = norms(x, s + 1)[2]
+        edge = jnp.where((row8 == s) & (col8 == s), d_refs[s][1, :8, :], edge_ref[...])
+        edge_ref[...] = jnp.where((row8 == s + 1) & (col8 == s), -length, edge)
+
+    def chain(s, k):
+        here, after, before = k + 1, k + 2, k
         old, new = s, s + 1
         d_prev, l_prev, d_now, l_now = d_refs[s], l_refs[s], d_refs[s + 1], l_refs[s + 1]
-        active = (k >= 0) & (k < steps)
-        limit = jnp.where(active, half, 0)
-        pick = jnp.where(active, new, -1)
-        x = x_refs[s][...]
-        d_old, l_old, d_next = d_prev[here], l_prev[here], d_prev[after]
+        active = k < steps
+        x = load(v_refs[s], here)
+        d_old, l_old, d_next = load(d_prev, here), load(l_prev, here), load(d_prev, after)
+        left = load(l_now, before)
         l_next = l_prev[after, old : old + 1, :]
-        left = l_now[before]
-
-        lead = jnp.where(lane == old, d_next[old : old + 1, :], l_old[old : old + 1, :])
-        lead_col = jnp.sum(
-            jnp.where(eye, jnp.broadcast_to(lead, (half, half)), 0.0), axis=1, keepdims=True
-        )
-        window = jnp.where(row == old, lead, jnp.where(col == old, lead_col, d_old))
-        rest_row = rest_ref[old : old + 1, :]
-        feed = jnp.where(k == steps - 2, half, 0)
-        corner = jnp.where(lane == old, l_next, jnp.where(lane < feed, rest_row, 0.0))
-        if s > 0:
-            rest_ref[...] = jnp.where(
-                col == jnp.where(k == steps - 1, old, -1), l_old, rest_ref[...]
-            )
-        below = jnp.where(row == old, corner, jnp.where(col == old, d_next, l_old))
-
-        rest = jnp.sum(jnp.where(row == new, 0.0, x * x), axis=0, keepdims=True)
-        top = x[new : new + 1, :]
-        length = jnp.sqrt(rest + top * top)
+        at_old, at_new = col8 == old, lane == new
+
+        x_row = tree([x[i] * eye_ref[8 * i : 8 * i + 8, :] for i in tiles])
+        rest, top, length = norms(x, new)
         v_top = top + length
         tau = 2.0 / (rest + v_top * v_top)
-        tau = jnp.where(lane < limit, tau, 0.0)
-        v_col = jnp.where(row < limit, jnp.where(row == new, v_top, x), 0.0)
-        v_row = jnp.sum(jnp.where(eye, v_col, 0.0), axis=0, keepdims=True)
-
-        beneath = jnp.sum(below * v_row, axis=1, keepdims=True)
-        beneath = jnp.where(row < limit, beneath * tau, 0.0)
-        first = k < 0
-        source = jnp.where(first, old, new)
-        head = jnp.where(row == old, l_next, d_next)
-        early = jnp.where(first, half, 0)
-        column = jnp.where(row < early, head, below)
-        column = jnp.sum(jnp.where(col == source, column, 0.0), axis=1, keepdims=True)
-        x_refs[s][...] = column - jnp.where(row < limit, beneath * v_top, 0.0)
-        below = below - beneath * v_row
-
-        inside = tau * jnp.sum(v_col * window, axis=0, keepdims=True)
-        scale = 0.5 * tau * jnp.sum(v_row * inside, axis=1, keepdims=True)
-        z_row = inside - scale * v_row
-        z_col = jnp.sum(
-            jnp.where(eye, jnp.broadcast_to(z_row, (half, half)), 0.0), axis=1, keepdims=True
-        )
-        window = window - v_col * z_row - z_col * v_row
-
-        across = tau * jnp.sum(v_col * left, axis=0, keepdims=True)
-        left = left - v_col * across
-        left = jnp.where(col == pick, jnp.where(row == new, -length, 0.0), left)
-
-        l_now[before] = left
-        d_now[here] = window
-        l_now[here] = below
-        v_refs[s][here] = v_col
+        tau = jnp.where(lane < jnp.where(active, half, 0), tau, 0.0)
+        v = [jnp.where(row8 == new, v_top, x[0])] + x[1:]
+        v_row = jnp.where(at_new, v_top, x_row)
+        tv_row = tau * v_row
+
+        corner = jnp.where(lane == old, l_next, 0.0)
+        for spot in range(1, s):
+            chosen = jnp.where(k == steps - 2, spot, -1)
+            corner = jnp.where(lane == chosen, l_refs[spot][steps, old : old + 1, :], corner)
+        below = [jnp.where(at_old, b, a) for a, b in zip(l_old, d_next)]
+        below[0] = jnp.where(row8 == old, corner, below[0])
+        column = [jnp.broadcast_to(a[:, new : new + 1], (8, half)) for a in below]
+        beneath = [jnp.sum(a * tv_row, axis=1, keepdims=True) for a in below]
+
+        lead = jnp.where(lane == old, d_next[0][old : old + 1, :], l_old[0][old : old + 1, :])
+        lead_col = [
+            jnp.sum(lead * eye_ref[8 * i : 8 * i + 8, :], axis=1, keepdims=True) for i in tiles
+        ]
+        window = [jnp.where(at_old, b, a) for a, b in zip(d_old, lead_col)]
+        window[0] = jnp.where(row8 == old, lead, window[0])
+        inside = tau * tree([a * b for a, b in zip(v, window)])
+        inside_col = [jnp.sum(a * tv_row, axis=1, keepdims=True) for a in window]
+        across = tau * tree([a * b for a, b in zip(v, left)])
+
+        store(v_refs[s], after, [c - b * v_top for c, b in zip(column, beneath)])
+        store(l_now, here, [a - b * v_row for a, b in zip(below, beneath)])
+        scale = jnp.sum(tv_row * inside, axis=1, keepdims=True)
+        mixed = inside - scale * v_row
+        store(d_now, here, [w - a * mixed - b * v_row for w, a, b in zip(window, v, inside_col)])
+        left = [w - a * across for w, a in zip(left, v)]
+        if s == sweeps - 1:
+            pick = col8 == jnp.where(active, new, -1)
+            left = [
+                jnp.where(pick, jnp.where(row8 == new, -length, 0.0) if i == 0 else 0.0, left[i])
+                for i in tiles
+            ]
+        store(l_now, before, left)
+        v_refs[s][here, :8, :] = v[0]
         tau_refs[s][here] = jnp.broadcast_to(tau, (8, half))
 
-        start = jnp.where(k == 0, s, -1)
-        edge = edge_ref[...]
-        edge = jnp.where((row8 == start) & (col8 == s), d_old[:8], edge)
-        below_start = jnp.where(k == 0, s + 1, -1)
-        edge = jnp.where((row8 == below_start) & (col8 == s), -length, edge)
-        edge_ref[...] = edge
-
-    def wave(t, carry):
-        for s in reversed(range(sweeps)):
-            chain(s, t)
-        return carry
-
-    lax.fori_loop(-1, blocks + LAG * (sweeps - 1), wave, 0)
+    def phase(first, last, chains):
+        def wave(t, carry):
+            for s in reversed(chains):
+                chain(s, t - LAG * s)
+            return carry
+
+        lax.fori_loop(first, last, wave, 0)
+
+    for s in range(sweeps - 1):
+        begin(s)
+        phase(LAG * s, LAG * (s + 1), range(s + 1))
+    begin(sweeps - 1)
+    phase(LAG * (sweeps - 1), blocks, range(sweeps))
+    for s in range(1, sweeps):
+        phase(blocks + LAG * (s - 1), blocks + LAG * s, range(s, sweeps))
 
     device = lax.axis_index("band")
     base = device * blocks_dev - halo
@@ -158,7 +182,9 @@
 
     d_last, l_last = d_refs[sweeps], l_refs[sweeps]
     edge = jnp.concatenate([edge_ref[...], zero[8:]], axis=0)
-    rest = rest_ref[...]
+    rest = zero
+    for s in range(1, sweeps):
+        rest = jnp.where(col == s, l_refs[s][steps], rest)
     d_last[0] = jnp.where(row < sweeps, edge, 0.0)
     l_last[0] = jnp.where(row >= sweeps, edge, 0.0)
     flip = jnp.where((row + col == half) | ((row == 0) & (col == 0)), 1.0, 0.0)
@@ -422,7 +448,6 @@
         [pltpu.VMEM((slots, half, half), f32)] * (2 * (sweeps + 1))
         + [pltpu.VMEM((slots, half, half), f32)] * sweeps
         + [pltpu.VMEM((slots, 8, half), f32)] * sweeps
-        + [pltpu.VMEM((half, half), f32)] * sweeps
         + [
             pltpu.VMEM((8, half), f32),
             pltpu.VMEM((half, half), f32),

time: 55 us -> 54.1 us (0.984)
  Pallas kernels: 54.2 us -> 53.3 us
    pallas_call x1, Pallas kernels: 27 us -> 26.1 us  [body(): pl.pallas_call(functools.partial(chase_kernel, blocks, half, blocks_dev,...]
where the time goes in v1:
time: 54.1 us; the launch traced here: 54 us
  Pallas kernels  53.3 us (99%)
  between operations  0.64 us (1%)
    pallas_call x1, Pallas kernels, body(): pl.pallas_call(functools.partial(gather_kernel, half, devices, cols, take...  27.3 us
    pallas_call x1, Pallas kernels, body(): pl.pallas_call(functools.partial(chase_kernel, blocks, half, blocks_dev,...  26.1 us

profile of v1, /device:TPU:25, one launch (start us, length us, event | category | flops | bytes accessed | tf_op | source)
XLA Modules:
  0.0 54.0 jit_solution(7110641174064218654)
XLA Ops:
  0.6 27.3 %shard_map.41 = (f32[8,136,384]{2,1,0:T(8,128)}, f32[512,128]{1,0:T(8,128)}, f32[8,128]{1,0:T(8,128)}) custom-call(f32[64,384]{1,0:T(8,128)} %band_ref.1, f32[384,128]{1,0:T(8,128)} %refs_2_.1), custom_call_target="tpu_custom_call" | custom-call | tf_op jit(solution)/shard_map/pallas_call | solution.py:420
  27.9 26.1 %shard_map.42 = (f32[64,384]{1,0:T(8,128)}, f32[384,128]{1,0:T(8,128)}) custom-call(f32[8,136,384]{2,1,0:T(8,128)} %get-tuple-element.5.refs_0_, f32[512,128]{1,0:T(8,128)} %get-tuple-element.6.refs_1_, f32[384,128]{1,0:T(8,128)} %refs_2_.1, f32[8,128]{1,0:T(8,128)} %get-tuple-element.7.refs_3_), custom_call_target="tpu_custom_call" | custom-call | tf_op jit(solution)/shard_map/pallas_call | solution.py:457

commit v2 on v0

--- a/solution.py
+++ b/solution.py
@@ -9,131 +9,165 @@
 
 SWEEPS = 4
 LAG = 3
+UNPACK = 2
 
 
 def chase_kernel(blocks, half, blocks_dev, halo, piece_count, sweeps, *refs):
     band_ref, above_ref, eig_ref, under_ref, band_out, eig_out = refs[:6]
-    refs = refs[2:]
-    d_refs = refs[4 : 5 + sweeps]
-    l_refs = refs[5 + sweeps : 6 + 2 * sweeps]
-    v_refs = refs[6 + 2 * sweeps : 6 + 3 * sweeps]
-    tau_refs = refs[6 + 3 * sweeps : 6 + 4 * sweeps]
-    x_refs = refs[6 + 4 * sweeps : 6 + 5 * sweeps]
-    edge_ref, rest_ref, turn_ref = refs[6 + 5 * sweeps :]
+    d_ref, l_ref, t_ref, eye_ref, edge_ref, raw_ref, turn_ref = refs[6:13]
+    v_refs = refs[13 : 13 + sweeps]
+    tau_refs = refs[13 + sweeps : 13 + 2 * sweeps]
+    last = sweeps - 1
+    pairs = [(a, b) for b in range(1, sweeps) for a in range(b)] + [(last, last)]
+    fields = dict(zip(pairs, refs[13 + 2 * sweeps :]))
     steps = blocks - 2
     row = lax.broadcasted_iota(jnp.int32, (half, half), 0)
     col = lax.broadcasted_iota(jnp.int32, (half, half), 1)
-    lane = lax.broadcasted_iota(jnp.int32, (1, half), 1)
     eye = row == col
     row8 = lax.broadcasted_iota(jnp.int32, (8, half), 0)
     col8 = lax.broadcasted_iota(jnp.int32, (8, half), 1)
     zero = jnp.zeros((half, half), jnp.float32)
-
-    def slot(k):
-        return jnp.clip(k, -1, blocks + 1) + 1
-
-    def unpack(block):
+    count = half // 8
+
+    def unpack(block, carry):
         dev = block // blocks_dev
         part = block % blocks_dev
         start = pl.multiple_of(part * half, half)
         piece = band_ref[dev, :half, pl.ds(start, half)]
         extra = band_ref[dev, half : half + 1, pl.ds(start, half)]
         rows = pltpu.roll(piece.T, 1, 1, stride=1, stride_axis=0)
-        d_refs[0][slot(block)] = jnp.where(row >= col, rows, rows.T)
-        l_refs[0][slot(block - 1)] = jnp.where(
-            col > row, rows, jnp.where(eye, jnp.broadcast_to(extra, (half, half)), 0.0)
-        )
-
-    def unpack_step(block, carry):
-        unpack(block)
+        turned = rows.T
+        extra = jnp.where(eye, jnp.broadcast_to(extra, (half, half)), 0.0)
+        d_ref[block + 2] = jnp.where(row >= col, rows, turned)
+        l_ref[block + 1] = jnp.where(col > row, rows, extra)
+        t_ref[block + 1] = jnp.where(row > col, turned, extra)
         return carry
 
-    lax.fori_loop(0, blocks, unpack_step, 0)
-    for extra_block in (blocks, blocks + 1):
-        d_refs[0][extra_block + 1] = zero
-    for extra_block in (blocks - 1, blocks, blocks + 1):
-        l_refs[0][extra_block + 1] = zero
-    edge_ref[...] = jnp.zeros(edge_ref.shape, jnp.float32)
-    rest_ref[...] = zero
-
-    def chain(s, t):
-        k = t - LAG * s
-        here, after, before = slot(k), slot(k + 1), slot(k - 1)
-        old, new = s, s + 1
-        d_prev, l_prev, d_now, l_now = d_refs[s], l_refs[s], d_refs[s + 1], l_refs[s + 1]
-        active = (k >= 0) & (k < steps)
-        limit = jnp.where(active, half, 0)
-        pick = jnp.where(active, new, -1)
-        x = x_refs[s][...]
-        d_old, l_old, d_next = d_prev[here], l_prev[here], d_prev[after]
-        l_next = l_prev[after, old : old + 1, :]
-        left = l_now[before]
-
-        lead = jnp.where(lane == old, d_next[old : old + 1, :], l_old[old : old + 1, :])
-        lead_col = jnp.sum(
-            jnp.where(eye, jnp.broadcast_to(lead, (half, half)), 0.0), axis=1, keepdims=True
-        )
-        window = jnp.where(row == old, lead, jnp.where(col == old, lead_col, d_old))
-        rest_row = rest_ref[old : old + 1, :]
-        feed = jnp.where(k == steps - 2, half, 0)
-        corner = jnp.where(lane == old, l_next, jnp.where(lane < feed, rest_row, 0.0))
-        if s > 0:
-            rest_ref[...] = jnp.where(
-                col == jnp.where(k == steps - 1, old, -1), l_old, rest_ref[...]
-            )
-        below = jnp.where(row == old, corner, jnp.where(col == old, d_next, l_old))
-
-        rest = jnp.sum(jnp.where(row == new, 0.0, x * x), axis=0, keepdims=True)
-        top = x[new : new + 1, :]
-        length = jnp.sqrt(rest + top * top)
+    lax.fori_loop(0, blocks, unpack, 0, unroll=UNPACK)
+    for spot in (0, 1, blocks + 2):
+        d_ref[spot] = zero
+    for spot in (0, blocks + 1):
+        l_ref[spot] = zero
+        t_ref[spot] = zero
+    for ref in v_refs + tau_refs + tuple(fields.values()) + (raw_ref, edge_ref):
+        ref[...] = jnp.zeros(ref.shape, jnp.float32)
+    eye_ref[...] = jnp.where(eye, 1.0, 0.0)
+
+    def tile(ref, k, i=0):
+        return ref[k + 2, 8 * i : 8 * i + 8, :]
+
+    def lanes(x):
+        return jnp.broadcast_to(jnp.sum(x, axis=1, keepdims=True), (8, half))
+
+    def rows_sum(x):
+        return jnp.broadcast_to(jnp.sum(x, axis=0, keepdims=True), (8, half))
+
+    def at_lane(x, spot):
+        return jnp.broadcast_to(x[:, spot : spot + 1], (8, half))
+
+    def total(parts):
+        while len(parts) > 1:
+            rest = parts[len(parts) // 2 * 2 :]
+            parts = [a + b for a, b in zip(parts[::2], parts[1::2])] + rest
+        return parts[0]
+
+    def to_lane(x, fill, spot):
+        return jnp.where(col8 == spot, fill, x)
+
+    def norms(x, new):
+        rest = lanes(to_lane(x * x, 0.0, new))
+        top = at_lane(x, new)
+        return rest, top, jnp.sqrt(rest + top * top)
+
+    def begin(s):
+        base = jnp.broadcast_to(d_ref[2, s : s + 1, :], (8, half))
+        x = jnp.where(col8 > s, base, jnp.broadcast_to(t_ref[2, s : s + 1, :], (8, half)))
+        diagonal = base
+        for a in range(s):
+            raw = raw_ref[a]
+            x = x - rows_sum(fields[a, s][2] * at_lane(raw, s))
+            diagonal = diagonal - 2.0 * raw[0:1, :] * raw[4:5, :]
+        length = norms(x, s + 1)[2]
+        edge = jnp.where((row8 == s) & (col8 == s), diagonal, edge_ref[...])
+        edge_ref[...] = jnp.where((row8 == s + 1) & (col8 == s), -length, edge)
+        return x, jnp.zeros((8, half), jnp.float32)
+
+    def chain(s, k, x, hung):
+        new = s + 1
+        main = col8 > s
+        x_col = [
+            jnp.sum(x * eye_ref[8 * i : 8 * i + 8, :], axis=1, keepdims=True) for i in range(count)
+        ]
+        rest, top, length = norms(x, new)
         v_top = top + length
         tau = 2.0 / (rest + v_top * v_top)
-        tau = jnp.where(lane < limit, tau, 0.0)
-        v_col = jnp.where(row < limit, jnp.where(row == new, v_top, x), 0.0)
-        v_row = jnp.sum(jnp.where(eye, v_col, 0.0), axis=0, keepdims=True)
-
-        beneath = jnp.sum(below * v_row, axis=1, keepdims=True)
-        beneath = jnp.where(row < limit, beneath * tau, 0.0)
-        first = k < 0
-        source = jnp.where(first, old, new)
-        head = jnp.where(row == old, l_next, d_next)
-        early = jnp.where(first, half, 0)
-        column = jnp.where(row < early, head, below)
-        column = jnp.sum(jnp.where(col == source, column, 0.0), axis=1, keepdims=True)
-        x_refs[s][...] = column - jnp.where(row < limit, beneath * v_top, 0.0)
-        below = below - beneath * v_row
-
-        inside = tau * jnp.sum(v_col * window, axis=0, keepdims=True)
-        scale = 0.5 * tau * jnp.sum(v_row * inside, axis=1, keepdims=True)
-        z_row = inside - scale * v_row
-        z_col = jnp.sum(
-            jnp.where(eye, jnp.broadcast_to(z_row, (half, half)), 0.0), axis=1, keepdims=True
-        )
-        window = window - v_col * z_row - z_col * v_row
-
-        across = tau * jnp.sum(v_col * left, axis=0, keepdims=True)
-        left = left - v_col * across
-        left = jnp.where(col == pick, jnp.where(row == new, -length, 0.0), left)
-
-        l_now[before] = left
-        d_now[here] = window
-        l_now[here] = below
-        v_refs[s][here] = v_col
-        tau_refs[s][here] = jnp.broadcast_to(tau, (8, half))
-
-        start = jnp.where(k == 0, s, -1)
-        edge = edge_ref[...]
-        edge = jnp.where((row8 == start) & (col8 == s), d_old[:8], edge)
-        below_start = jnp.where(k == 0, s + 1, -1)
-        edge = jnp.where((row8 == below_start) & (col8 == s), -length, edge)
-        edge_ref[...] = edge
-
-    def wave(t, carry):
-        for s in reversed(range(sweeps)):
-            chain(s, t)
-        return carry
-
-    lax.fori_loop(-1, blocks + LAG * (sweeps - 1), wave, 0)
+        v = to_lane(x, v_top, new)
+        v_first = jnp.where(row8 == new, v_top, x_col[0])
+        v_main = jnp.where(row8 > s, v_first, 0.0)
+        v_tail = v_first - v_main
+
+        def times(ref, spot, extra):
+            parts = [tile(ref, spot, i) * x_col[i] for i in range(1, count)]
+            return total(parts) + tile(ref, spot) * v_main + extra
+
+        here = times(d_ref, k, tile(l_ref, k) * v_tail)
+        after = times(t_ref, k, tile(d_ref, k + 1) * v_tail)
+        beyond = tile(t_ref, k + 1) * v_tail
+        before = times(l_ref, k - 1, 0.0)
+        inside = jnp.where(main, here, after)
+        beneath = jnp.where(main, after, beyond)
+        across = jnp.where(main, before, here)
+        across = across - jnp.where(row8 == 0, v_refs[s][k] * (lanes(hung * x) + length * at_lane(hung, new)), 0.0)
+        column = jnp.where(main, jnp.broadcast_to(t_ref[k + 2, new : new + 1, :], (8, half)), 0.0)
+        fixes = []
+        for a in range(s):
+            now = fields[a, s][k + 2]
+            up = jnp.where(row8 == 1, 0.0, fields[a, s][k + 1])
+            down = jnp.where(row8 == 2, 0.0, fields[a, s][k + 3])
+            unit = at_lane(now, new)
+            dots = lanes(now * x) + length * unit
+            inside = inside - now * pltpu.roll(dots, 4, 0)
+            beneath = beneath - down * pltpu.roll(dots, 1, 0)
+            across = across - up * pltpu.roll(dots, 7, 0)
+            fixes.append(down * pltpu.roll(unit, 1, 0))
+        inside = tau * rows_sum(inside)
+        beneath = tau * rows_sum(beneath)
+        across = tau * rows_sum(across)
+        if fixes:
+            column = column - rows_sum(total(fixes))
+        inside = inside - 0.5 * tau * lanes(v * inside) * v
+
+        v_refs[s][k + 1] = v
+        tau_refs[s][k + 1] = tau
+        for b in range(s + 1, sweeps) if s < last else (last,):
+            ref = fields[s, b]
+            other = (col8 > s) & (col8 <= b)
+            ref[k + 2, 0:1, :] = jnp.where(other, 0.0, v)[0:1]
+            ref[k + 2, 4:5, :] = jnp.where(other, beneath, inside)[0:1]
+            ref[k + 1, 7:8, :] = jnp.where(other, inside, across)[0:1]
+            ref[k + 3, 1:2, :] = jnp.where(other, 0.0, beneath)[0:1]
+            if b > s:
+                ref[k + 1, 3:4, :] = jnp.where(other, v, 0.0)[0:1]
+                ref[k, 2:3, :] = jnp.where(other, across, 0.0)[0:1]
+        if s < last:
+            raw_ref[s, 0:1, :] = jnp.where(col8 < jnp.where(k == 0, half, 0), inside, raw_ref[s])[0:1]
+            raw_ref[s, 3:4, :] = jnp.where(col8 < jnp.where(k == 1, half, 0), across, raw_ref[s])[3:4]
+            raw_ref[s, 4:5, :] = jnp.where(col8 < jnp.where(k == 0, half, 0), v, raw_ref[s])[4:5]
+        return column - beneath * v_top, beneath
+
+    def phase(start, stop, chains, xs):
+        def wave(t, xs):
+            done = {s: chain(s, t - LAG * s, *x) for s, x in reversed(list(zip(chains, xs)))}
+            return tuple(done[s] for s in chains)
+
+        return lax.fori_loop(start, stop, wave, tuple(xs))
+
+    xs = ()
+    for s in range(last):
+        xs = phase(LAG * s, LAG * (s + 1), range(s + 1), xs + (begin(s),))
+    xs = phase(LAG * last, steps, range(sweeps), xs + (begin(last),))
+    for s in range(1, sweeps):
+        xs = phase(steps + LAG * (s - 1), steps + LAG * s, range(s, sweeps), xs[1:])
 
     device = lax.axis_index("band")
     base = device * blocks_dev - halo
@@ -143,9 +177,9 @@
     for s in reversed(range(sweeps)):
         lead_rows = s + 1
         for e in range(sweeps - 1 - s + halo - sweeps, halo + blocks_dev):
-            k = base + e
-            v = v_refs[s][slot(k)]
-            tau = tau_refs[s][slot(k), 0:1, :]
+            spot = jnp.clip(base + e, -1, blocks - 1) + 1
+            v = jnp.sum(v_refs[s][spot, 0:1, :] * eye_ref[...], axis=1, keepdims=True)
+            tau = tau_refs[s][spot, 0:1, :]
             low, high = eig[e], eig[e + 1]
             mixed = jnp.concatenate([jnp.where(row8 < lead_rows, high[:8], low[:8]), low[8:]], 0)
             inner = tau * jnp.sum(v * mixed, axis=0, keepdims=True)
@@ -156,20 +190,53 @@
     for m in range(blocks_dev):
         eig_out[m * half : (m + 1) * half, :] = eig[halo + m]
 
-    d_last, l_last = d_refs[sweeps], l_refs[sweeps]
+    def product(a, b):
+        return lax.dot_general(
+            a, b, (((0,), (0,)), ((), ())),
+            precision=lax.Precision.HIGHEST, preferred_element_type=jnp.float32,
+        )
+
+    def stack(k, shift=0, drop=None):
+        parts = []
+        for a in range(sweeps):
+            part = fields[a, last][k + 2]
+            part = part if drop is None else jnp.where(row8 == drop, 0.0, part)
+            parts.append(pltpu.roll(part, shift, 0) if shift else part)
+        return jnp.concatenate(parts, 0)
+
+    def final_d(k):
+        outer = jnp.where(col > last, d_ref[k + 2], t_ref[k + 2])
+        inner = jnp.where(col > last, l_ref[k + 2], d_ref[k + 3])
+        return jnp.where(row > last, outer, inner) - product(stack(k), stack(k, 4))
+
+    def final_l(k):
+        outer = jnp.where(col > last, l_ref[k + 2], d_ref[k + 3])
+        inner = jnp.where(col > last, 0.0, l_ref[k + 3])
+        block = jnp.where(row > last, outer, inner) - product(stack(k + 1, 0, 2), stack(k, 1))
+        cleared = jnp.where(k <= steps - 2, sweeps, -1)
+        return jnp.where((col == cleared) & (row != sweeps), 0.0, block)
+
     edge = jnp.concatenate([edge_ref[...], zero[8:]], axis=0)
-    rest = rest_ref[...]
-    d_last[0] = jnp.where(row < sweeps, edge, 0.0)
-    l_last[0] = jnp.where(row >= sweeps, edge, 0.0)
+    bottom, lead = [], []
+    for a in range(last):
+        bottom.append(jnp.where(row8 == 1, fields[a, last][steps + 2], 0.0))
+        lead.append(pltpu.roll(jnp.where(row8 == 3, fields[a, last][steps], 0.0), 6, 0))
+    rest = -product(jnp.concatenate(bottom, 0), jnp.concatenate(lead, 0))
     flip = jnp.where((row + col == half) | ((row == 0) & (col == 0)), 1.0, 0.0)
     position = lax.axis_index("cols") * piece_count
+    first = device * blocks_dev
+    d_last = [final_d(first + m - 1) for m in range(blocks_dev + 1)]
+    l_last = [final_l(first + m - 2) for m in range(blocks_dev + 1)]
+    top = jnp.where(device == 0, half, 0)
+    d_last[0] = jnp.where(row < top, jnp.where(row < sweeps, edge, 0.0), d_last[0])
+    l_last[1] = jnp.where(row < top, jnp.where(row >= sweeps, edge, 0.0), l_last[1])
     for m in range(blocks_dev):
-        b = device * blocks_dev + m
+        b = first + m
         lim = jnp.where(b > 0, half, 0)
         rest_below = jnp.where(b == steps, half, 0)
         rest_last = jnp.where(b == steps + 1, half, 0)
-        d_here, d_before = d_last[slot(b)], d_last[slot(b - 1)]
-        l_here, l_before = l_last[slot(b - 1)], l_last[slot(b - 2)]
+        d_here, d_before = d_last[m + 1], d_last[m]
+        l_here, l_before = l_last[m + 1], l_last[m]
         c0 = jnp.where(
             row >= sweeps, jnp.where(col >= sweeps, d_here, l_here), jnp.where(col < sweeps, d_before, 0.0)
         )
@@ -417,17 +484,18 @@
         compiler_params=pltpu.CompilerParams(collective_id=0, has_side_effects=True),
     )(band_diagonals, eigenvectors)
 
-    slots = blocks + 3
+    slots = blocks + 4
+    pair_count = sweeps * (sweeps - 1) // 2 + 1
     scratch = (
-        [pltpu.VMEM((slots, half, half), f32)] * (2 * (sweeps + 1))
-        + [pltpu.VMEM((slots, half, half), f32)] * sweeps
-        + [pltpu.VMEM((slots, 8, half), f32)] * sweeps
-        + [pltpu.VMEM((half, half), f32)] * sweeps
+        [pltpu.VMEM((slots, half, half), f32)] * 3
         + [
+            pltpu.VMEM((half, half), f32),
             pltpu.VMEM((8, half), f32),
-            pltpu.VMEM((half, half), f32),
+            pltpu.VMEM((sweeps, 8, half), f32),
             pltpu.VMEM((double, half), f32),
         ]
+        + [pltpu.VMEM((blocks + 1, 8, half), f32)] * (2 * sweeps)
+        + [pltpu.VMEM((slots, 8, half), f32)] * pair_count
     )
     return pl.pallas_call(
         functools.partial(chase_kernel, blocks, half, blocks_dev, halo, piece_count, sweeps),

time: 55 us -> 47.9 us (0.87)
  Pallas kernels: 54.2 us -> 47.1 us
    pallas_call x1, Pallas kernels: 27 us -> 19.9 us  [body(): pl.pallas_call(functools.partial(chase_kernel, blocks, half, blocks_dev,...]
where the time goes in v2:
time: 47.9 us; the launch traced here: 47.8 us
  Pallas kernels  47.1 us (98%)
  between operations  0.64 us (1%)
    pallas_call x1, Pallas kernels, body(): pl.pallas_call(functools.partial(gather_kernel, half, devices, cols, take...  27.3 us
    pallas_call x1, Pallas kernels, body(): pl.pallas_call(functools.partial(chase_kernel, blocks, half, blocks_dev,...  19.9 us

profile of v2, /device:TPU:25, one launch (start us, length us, event | category | flops | bytes accessed | tf_op | source)
XLA Modules:
  0.0 47.8 jit_solution(11725095585393896096)
XLA Ops:
  0.6 27.3 %shard_map.41 = (f32[8,136,384]{2,1,0:T(8,128)}, f32[512,128]{1,0:T(8,128)}, f32[8,128]{1,0:T(8,128)}) custom-call(f32[64,384]{1,0:T(8,128)} %band_ref.1, f32[384,128]{1,0:T(8,128)} %refs_2_.1), custom_call_target="tpu_custom_call" | custom-call | tf_op jit(solution)/shard_map/pallas_call | solution.py:461
  27.9 19.9 %shard_map.42 = (f32[64,384]{1,0:T(8,128)}, f32[384,128]{1,0:T(8,128)}) custom-call(f32[8,136,384]{2,1,0:T(8,128)} %get-tuple-element.5.refs_0_, f32[512,128]{1,0:T(8,128)} %get-tuple-element.6.refs_1_, f32[384,128]{1,0:T(8,128)} %refs_2_.1, f32[8,128]{1,0:T(8,128)} %get-tuple-element.7.refs_3_), custom_call_target="tpu_custom_call" | custom-call | tf_op jit(solution)/shard_map/pallas_call | solution.py:500

commit v3 on v2

--- a/solution.py
+++ b/solution.py
@@ -9,7 +9,8 @@
 
 SWEEPS = 4
 LAG = 3
-UNPACK = 2
+AHEAD = 4
+UNROLL = 2
 
 
 def chase_kernel(blocks, half, blocks_dev, halo, piece_count, sweeps, *refs):
@@ -29,7 +30,7 @@
     zero = jnp.zeros((half, half), jnp.float32)
     count = half // 8
 
-    def unpack(block, carry):
+    def unpack(block):
         dev = block // blocks_dev
         part = block % blocks_dev
         start = pl.multiple_of(part * half, half)
@@ -41,9 +42,7 @@
         d_ref[block + 2] = jnp.where(row >= col, rows, turned)
         l_ref[block + 1] = jnp.where(col > row, rows, extra)
         t_ref[block + 1] = jnp.where(row > col, turned, extra)
-        return carry
-
-    lax.fori_loop(0, blocks, unpack, 0, unroll=UNPACK)
+
     for spot in (0, 1, blocks + 2):
         d_ref[spot] = zero
     for spot in (0, blocks + 1):
@@ -77,11 +76,16 @@
     def norms(x, new):
         rest = lanes(to_lane(x * x, 0.0, new))
         top = at_lane(x, new)
-        return rest, top, jnp.sqrt(rest + top * top)
+        square = rest + top * top
+        inverse = lax.rsqrt(square)
+        return rest, top, square * inverse, inverse
+
+    def wide(line):
+        return jnp.broadcast_to(line, (8, half))
 
     def begin(s):
-        base = jnp.broadcast_to(d_ref[2, s : s + 1, :], (8, half))
-        x = jnp.where(col8 > s, base, jnp.broadcast_to(t_ref[2, s : s + 1, :], (8, half)))
+        base = wide(d_ref[2, s : s + 1, :])
+        x = jnp.where(col8 > s, base, wide(t_ref[2, s : s + 1, :]))
         diagonal = base
         for a in range(s):
             raw = raw_ref[a]
@@ -90,84 +94,111 @@
         length = norms(x, s + 1)[2]
         edge = jnp.where((row8 == s) & (col8 == s), diagonal, edge_ref[...])
         edge_ref[...] = jnp.where((row8 == s + 1) & (col8 == s), -length, edge)
-        return x, jnp.zeros((8, half), jnp.float32)
-
-    def chain(s, k, x, hung):
+        return (x,) + (jnp.zeros((8, half), jnp.float32),) * 4
+
+    def targets(s):
+        return range(s + 1, sweeps) if s < last else (last,)
+
+    def settle(s, k, inside, v, tau):
+        inside = inside - 0.5 * tau * lanes(v * inside) * v
+        for b in targets(s):
+            ref = fields[s, b]
+            other = (col8 > s) & (col8 <= b)
+            ref[k + 2, 4:5, :] = jnp.where(other, wide(ref[k + 2, 4:5, :]), inside)[0:1]
+            if b > s:
+                ref[k + 1, 7:8, :] = jnp.where(other, inside, wide(ref[k + 1, 7:8, :]))[0:1]
+        if s < last:
+            raw_ref[s, 0:1, :] = jnp.where(col8 < jnp.where(k == 0, half, 0), inside, wide(raw_ref[s, 0:1, :]))[0:1]
+
+    def chain(s, k, x, hung, inside_past, v_past, tau_past):
         new = s + 1
         main = col8 > s
         x_col = [
             jnp.sum(x * eye_ref[8 * i : 8 * i + 8, :], axis=1, keepdims=True) for i in range(count)
         ]
-        rest, top, length = norms(x, new)
-        v_top = top + length
-        tau = 2.0 / (rest + v_top * v_top)
-        v = to_lane(x, v_top, new)
-        v_first = jnp.where(row8 == new, v_top, x_col[0])
-        v_main = jnp.where(row8 > s, v_first, 0.0)
-        v_tail = v_first - v_main
+        rest, top, length, inverse = norms(x, new)
+        x_main = jnp.where(row8 > s, x_col[0], 0.0)
+        x_tail = jnp.where(row8 > s, 0.0, x_col[0])
 
         def times(ref, spot, extra):
             parts = [tile(ref, spot, i) * x_col[i] for i in range(1, count)]
-            return total(parts) + tile(ref, spot) * v_main + extra
-
-        here = times(d_ref, k, tile(l_ref, k) * v_tail)
-        after = times(t_ref, k, tile(d_ref, k + 1) * v_tail)
-        beyond = tile(t_ref, k + 1) * v_tail
-        before = times(l_ref, k - 1, 0.0)
+            return total(parts + [tile(ref, spot) * x_main] + extra)
+
+        here = times(d_ref, k, [tile(l_ref, k) * x_tail])
+        after = times(t_ref, k, [tile(d_ref, k + 1) * x_tail])
+        beyond = tile(t_ref, k + 1) * x_tail
+        before = times(l_ref, k - 1, [])
+        here_top = wide(d_ref[k + 2, new : new + 1, :])
+        after_top = wide(t_ref[k + 2, new : new + 1, :])
+        before_top = wide(l_ref[k + 1, new : new + 1, :])
         inside = jnp.where(main, here, after)
         beneath = jnp.where(main, after, beyond)
         across = jnp.where(main, before, here)
-        across = across - jnp.where(row8 == 0, v_refs[s][k] * (lanes(hung * x) + length * at_lane(hung, new)), 0.0)
-        column = jnp.where(main, jnp.broadcast_to(t_ref[k + 2, new : new + 1, :], (8, half)), 0.0)
         fixes = []
         for a in range(s):
             now = fields[a, s][k + 2]
             up = jnp.where(row8 == 1, 0.0, fields[a, s][k + 1])
             down = jnp.where(row8 == 2, 0.0, fields[a, s][k + 3])
             unit = at_lane(now, new)
-            dots = lanes(now * x) + length * unit
+            dots = lanes(now * x)
+            beneath = beneath - down * pltpu.roll(dots, 1, 0)
+            fixes.append(down * pltpu.roll(unit, 1, 0))
+            dots = dots + length * unit
             inside = inside - now * pltpu.roll(dots, 4, 0)
-            beneath = beneath - down * pltpu.roll(dots, 1, 0)
             across = across - up * pltpu.roll(dots, 7, 0)
-            fixes.append(down * pltpu.roll(unit, 1, 0))
-        inside = tau * rows_sum(inside)
-        beneath = tau * rows_sum(beneath)
-        across = tau * rows_sum(across)
+        beneath = rows_sum(beneath)
+        x_next = beneath * -inverse
+        column = jnp.where(main, after_top, 0.0)
         if fixes:
             column = column - rows_sum(total(fixes))
-        inside = inside - 0.5 * tau * lanes(v * inside) * v
-
+        hang = lanes(hung * x) + length * at_lane(hung, new)
+        v_top = top + length
+        tau = 2.0 / (rest + v_top * v_top)
+        v = to_lane(x, v_top, new)
+        beneath = tau * (beneath + length * column)
+        inside = tau * (rows_sum(inside) + length * jnp.where(main, here_top, after_top))
+        across = tau * (rows_sum(across) + length * jnp.where(main, before_top, here_top) - v_past * hang)
+
+        settle(s, k - 1, inside_past, v_past, tau_past)
         v_refs[s][k + 1] = v
         tau_refs[s][k + 1] = tau
-        for b in range(s + 1, sweeps) if s < last else (last,):
+        for b in targets(s):
             ref = fields[s, b]
             other = (col8 > s) & (col8 <= b)
             ref[k + 2, 0:1, :] = jnp.where(other, 0.0, v)[0:1]
-            ref[k + 2, 4:5, :] = jnp.where(other, beneath, inside)[0:1]
-            ref[k + 1, 7:8, :] = jnp.where(other, inside, across)[0:1]
+            ref[k + 1, 7:8, :] = across[0:1]
             ref[k + 3, 1:2, :] = jnp.where(other, 0.0, beneath)[0:1]
             if b > s:
+                ref[k + 2, 4:5, :] = beneath[0:1]
                 ref[k + 1, 3:4, :] = jnp.where(other, v, 0.0)[0:1]
                 ref[k, 2:3, :] = jnp.where(other, across, 0.0)[0:1]
         if s < last:
-            raw_ref[s, 0:1, :] = jnp.where(col8 < jnp.where(k == 0, half, 0), inside, raw_ref[s])[0:1]
-            raw_ref[s, 3:4, :] = jnp.where(col8 < jnp.where(k == 1, half, 0), across, raw_ref[s])[3:4]
-            raw_ref[s, 4:5, :] = jnp.where(col8 < jnp.where(k == 0, half, 0), v, raw_ref[s])[4:5]
-        return column - beneath * v_top, beneath
-
-    def phase(start, stop, chains, xs):
-        def wave(t, xs):
-            done = {s: chain(s, t - LAG * s, *x) for s, x in reversed(list(zip(chains, xs)))}
+            raw_ref[s, 3:4, :] = jnp.where(col8 < jnp.where(k == 1, half, 0), across, wide(raw_ref[s, 3:4, :]))[0:1]
+            raw_ref[s, 4:5, :] = jnp.where(col8 < jnp.where(k == 0, half, 0), v, wide(raw_ref[s, 4:5, :]))[0:1]
+        return x_next, beneath, inside, v, tau
+
+    def phase(start, stop, chains, states):
+        def wave(t, states):
+            done = {s: chain(s, t - LAG * s, *state) for s, state in reversed(list(zip(chains, states)))}
+            if start < steps:
+                unpack(jnp.minimum(t + AHEAD, blocks - 1))
             return tuple(done[s] for s in chains)
 
-        return lax.fori_loop(start, stop, wave, tuple(xs))
-
-    xs = ()
+        return lax.fori_loop(start, stop, wave, tuple(states), unroll=UNROLL)
+
+    def drain(s, state):
+        settle(s, steps - 1, *state[2:])
+
+    for block in range(AHEAD):
+        unpack(block)
+    states = ()
     for s in range(last):
-        xs = phase(LAG * s, LAG * (s + 1), range(s + 1), xs + (begin(s),))
-    xs = phase(LAG * last, steps, range(sweeps), xs + (begin(last),))
+        states = phase(LAG * s, LAG * (s + 1), range(s + 1), states + (begin(s),))
+    states = phase(LAG * last, steps, range(sweeps), states + (begin(last),))
     for s in range(1, sweeps):
-        xs = phase(steps + LAG * (s - 1), steps + LAG * s, range(s, sweeps), xs[1:])
+        drain(s - 1, states[0])
+        states = phase(steps + LAG * (s - 1), steps + LAG * s, range(s, sweeps), states[1:])
+    drain(last, states[0])
 
     device = lax.axis_index("band")
     base = device * blocks_dev - halo

time: 47.9 us -> 42 us (0.88)
  Pallas kernels: 47.1 us -> 41.2 us
    pallas_call x1, Pallas kernels: 19.9 us -> 14 us  [body(): pl.pallas_call(functools.partial(chase_kernel, blocks, half, blocks_dev,...]
where the time goes in v3:
time: 42 us; the launch traced here: 41.9 us
  Pallas kernels  41.2 us (98%)
  between operations  0.64 us (2%)
    pallas_call x1, Pallas kernels, body(): pl.pallas_call(functools.partial(gather_kernel, half, devices, cols, take...  27.3 us
    pallas_call x1, Pallas kernels, body(): pl.pallas_call(functools.partial(chase_kernel, blocks, half, blocks_dev,...  14 us

profile of v3, /device:TPU:25, one launch (start us, length us, event | category | flops | bytes accessed | tf_op | source)
XLA Modules:
  0.0 41.9 jit_solution(17271901025590714971)
XLA Ops:
  0.6 27.3 %shard_map.41 = (f32[8,136,384]{2,1,0:T(8,128)}, f32[512,128]{1,0:T(8,128)}, f32[8,128]{1,0:T(8,128)}) custom-call(f32[64,384]{1,0:T(8,128)} %band_ref.1, f32[384,128]{1,0:T(8,128)} %refs_2_.1), custom_call_target="tpu_custom_call" | custom-call | tf_op jit(solution)/shard_map/pallas_call | solution.py:492
  27.9 14.0 %shard_map.42 = (f32[64,384]{1,0:T(8,128)}, f32[384,128]{1,0:T(8,128)}) custom-call(f32[8,136,384]{2,1,0:T(8,128)} %get-tuple-element.5.refs_0_, f32[512,128]{1,0:T(8,128)} %get-tuple-element.6.refs_1_, f32[384,128]{1,0:T(8,128)} %refs_2_.1, f32[8,128]{1,0:T(8,128)} %get-tuple-element.7.refs_3_), custom_call_target="tpu_custom_call" | custom-call | tf_op jit(solution)/shard_map/pallas_call | solution.py:531

commit v4 on v3

--- a/solution.py
+++ b/solution.py
@@ -10,17 +10,20 @@
 SWEEPS = 4
 LAG = 3
 AHEAD = 4
+EARLY = 3
 UNROLL = 2
 
 
-def chase_kernel(blocks, half, blocks_dev, halo, piece_count, sweeps, *refs):
-    band_ref, above_ref, eig_ref, under_ref, band_out, eig_out = refs[:6]
-    d_ref, l_ref, t_ref, eye_ref, edge_ref, raw_ref, turn_ref = refs[6:13]
-    v_refs = refs[13 : 13 + sweeps]
-    tau_refs = refs[13 + sweeps : 13 + 2 * sweeps]
+def kernel(half, devices, cols, takes, blocks, halo, sweeps, band_in, eig_ref, band_out, eig_out, *refs):
+    all_ref, above_ref, under_ref, rev_ref, sems = refs[:5]
+    refs = refs[5:]
+    d_ref, l_ref, t_ref, eye_ref, edge_ref, raw_ref, turn_ref = refs[:7]
+    v_refs = refs[7 : 7 + sweeps]
+    tau_refs = refs[7 + sweeps : 7 + 2 * sweeps]
     last = sweeps - 1
     pairs = [(a, b) for b in range(1, sweeps) for a in range(b)] + [(last, last)]
-    fields = dict(zip(pairs, refs[13 + 2 * sweeps :]))
+    fields = dict(zip(pairs, refs[7 + 2 * sweeps :]))
+    piece_count, blocks_dev = band_in.shape[0], band_in.shape[1] // half
     steps = blocks - 2
     row = lax.broadcasted_iota(jnp.int32, (half, half), 0)
     col = lax.broadcasted_iota(jnp.int32, (half, half), 1)
@@ -30,18 +33,28 @@
     zero = jnp.zeros((half, half), jnp.float32)
     count = half // 8
 
-    def unpack(block):
-        dev = block // blocks_dev
-        part = block % blocks_dev
-        start = pl.multiple_of(part * half, half)
-        piece = band_ref[dev, :half, pl.ds(start, half)]
-        extra = band_ref[dev, half : half + 1, pl.ds(start, half)]
-        rows = pltpu.roll(piece.T, 1, 1, stride=1, stride_axis=0)
-        turned = rows.T
-        extra = jnp.where(eye, jnp.broadcast_to(extra, (half, half)), 0.0)
-        d_ref[block + 2] = jnp.where(row >= col, rows, turned)
-        l_ref[block + 1] = jnp.where(col > row, rows, extra)
-        t_ref[block + 1] = jnp.where(row > col, turned, extra)
+    z_send, z_recv, own_sem, x_send, x_recv, p_send, p_recv, e_send, e_recv = sems
+    d, c = lax.axis_index("band"), lax.axis_index("cols")
+    deep, rows_dev = band_in.shape
+    full = half // deep
+    pieces = full + 1
+    parts = rows_dev // half
+    chips = devices // 2
+    chip, core = d // 2, d % 2
+    partner = chip * 2 + 1 - core
+
+    barrier = pltpu.get_barrier_semaphore()
+    peers = [(d, (c + hop) % cols) for hop in range(1, cols)]
+    peers += [((chip + hop) % chips * 2 + core, c) for hop in range(1, chips)]
+    peers.append((partner, c))
+    for hop in range(1, len(takes) + 1):
+        peers += [((d + hop) % devices, c), ((d - hop + devices) % devices, c)]
+    for peer in peers:
+        pl.semaphore_signal(barrier, inc=1, device_id=peer, device_id_type=pl.DeviceIdType.MESH)
+
+    for r in range(deep):
+        for m in range(parts):
+            rev_ref[m, r : r + 1, :] = band_in[deep - 1 - r : deep - r, m * half : (m + 1) * half]
 
     for spot in (0, 1, blocks + 2):
         d_ref[spot] = zero
@@ -51,6 +64,126 @@
     for ref in v_refs + tau_refs + tuple(fields.values()) + (raw_ref, edge_ref):
         ref[...] = jnp.zeros(ref.shape, jnp.float32)
     eye_ref[...] = jnp.where(eye, 1.0, 0.0)
+
+    pl.semaphore_wait(barrier, len(peers))
+
+    def send(src, dst, send_sem, recv_sem, device):
+        return pltpu.make_async_remote_copy(
+            src_ref=src,
+            dst_ref=dst,
+            send_sem=send_sem,
+            recv_sem=recv_sem,
+            device_id=device,
+            device_id_type=pl.DeviceIdType.MESH,
+        )
+
+    def rows_of(p):
+        return pl.ds(half - (p + 1) * deep, deep) if p < full else pl.ds(half, 8)
+
+    def source(p, m):
+        return rev_ref.at[m] if p < full else band_in.at[pl.ds(0, 8), pl.ds(m * half, half)]
+
+    def place(p, m):
+        return all_ref.at[d * parts + m, rows_of(p)]
+
+    def along(p, m, to):
+        return send(source(p, m), place(p, m), z_send.at[m, to], z_recv.at[p, m], (d, to))
+
+    def own(p, m):
+        return pltpu.make_async_copy(source(p, m), place(p, m), own_sem.at[m])
+
+    def chunk(owner, m):
+        return all_ref.at[owner * parts + m]
+
+    def across(to, m):
+        src = chunk(d, m)
+        return send(src, src, x_send.at[to, m], x_recv.at[chip, m], (to * 2 + core, c))
+
+    def arrived(owner, m):
+        src = chunk(owner * 2 + core, m)
+        return send(src, src, x_send.at[owner, m], x_recv.at[owner, m], (owner * 2 + core, c))
+
+    def share(owner, m):
+        src = chunk(owner * 2 + core, m)
+        return send(src, src, p_send.at[owner, m], p_recv.at[owner, m], (partner, c))
+
+    halos = []
+    end = sum(takes)
+    for hop, take in enumerate(takes, 1):
+        halos.append(
+            send(
+                eig_ref.at[pl.ds(rows_dev - take, take)],
+                above_ref.at[pl.ds(end - take, take)],
+                e_send.at[hop],
+                e_recv.at[hop],
+                ((d + hop) % devices, c),
+            )
+        )
+        end -= take
+    halos.append(
+        send(eig_ref.at[pl.ds(0, 8)], under_ref, e_send.at[0], e_recv.at[0], ((d - 1 + devices) % devices, c))
+    )
+
+    for p in range(pieces):
+
+        @pl.when(c == p)
+        def _():
+            for m in range(parts):
+                for to in reversed(range(cols)):
+                    if to != p:
+                        along(p, m, to).start()
+                own(p, m).start()
+
+    for copy in halos:
+        copy.start()
+
+    for m in range(parts):
+        for p in range(pieces):
+
+            @pl.when(c == p)
+            def _():
+                own(p, m).wait()
+
+            @pl.when(c != p)
+            def _():
+                along(p, m, c).wait_recv()
+
+        for to in reversed(range(chips)):
+
+            @pl.when(chip != to)
+            def _():
+                across(to, m).start()
+
+        share(chip, m).start()
+
+    def sides(block):
+        owner, m = block // parts, block % parts
+        return owner // 2, owner % 2, m
+
+    def duty(block):
+        owner, side, m = sides(block)
+
+        @pl.when((side == core) & (owner != chip) & (block < blocks))
+        def _():
+            arrived(owner, m).wait_recv()
+            share(owner, m).start()
+
+    def need(block):
+        owner, side, m = sides(block)
+
+        @pl.when((side != core) & (block < blocks))
+        def _():
+            share(owner, m).wait_recv()
+
+    def unpack(block):
+        piece = all_ref[block, :half]
+        extra = all_ref[block, half : half + 1]
+        rows = pltpu.roll(piece.T, 1, 1, stride=1, stride_axis=0)
+        turned = rows.T
+        extra = jnp.where(eye, jnp.broadcast_to(extra, (half, half)), 0.0)
+        d_ref[block + 2] = jnp.where(row >= col, rows, turned)
+        l_ref[block + 1] = jnp.where(col > row, rows, extra)
+        t_ref[block + 1] = jnp.where(row > col, turned, extra)
 
     def tile(ref, k, i=0):
         return ref[k + 2, 8 * i : 8 * i + 8, :]
@@ -184,12 +317,30 @@
                 unpack(jnp.minimum(t + AHEAD, blocks - 1))
             return tuple(done[s] for s in chains)
 
-        return lax.fori_loop(start, stop, wave, tuple(states), unroll=UNROLL)
+        def turn(t, states, size):
+            if start < steps:
+                for more in range(size):
+                    duty(t + more + AHEAD + EARLY)
+                for more in range(size):
+                    need(t + more + AHEAD)
+            for more in range(size):
+                states = wave(t + more, states)
+            return states
+
+        size = min(UNROLL, stop - start)
+        turns = (stop - start) // size
+        states = lax.fori_loop(0, turns, lambda i, st: turn(start + i * size, st, size), tuple(states))
+        if start + turns * size < stop:
+            states = turn(start + turns * size, states, stop - start - turns * size)
+        return states
 
     def drain(s, state):
         settle(s, steps - 1, *state[2:])
 
+    for block in range(AHEAD + EARLY):
+        duty(block)
     for block in range(AHEAD):
+        need(block)
         unpack(block)
     states = ()
     for s in range(last):
@@ -199,6 +350,25 @@
         drain(s - 1, states[0])
         states = phase(steps + LAG * (s - 1), steps + LAG * s, range(s, sweeps), states[1:])
     drain(last, states[0])
+
+    for m in range(parts):
+        for p in range(pieces):
+
+            @pl.when(c == p)
+            def _():
+                for to in range(cols):
+                    if to != p:
+                        along(p, m, to).wait_send()
+
+        for owner in range(chips):
+
+            @pl.when(chip != owner)
+            def _():
+                across(owner, m).wait_send()
+
+            share(owner, m).wait_send()
+    for copy in halos:
+        copy.wait()
 
     device = lax.axis_index("band")
     base = device * blocks_dev - halo
@@ -289,187 +459,6 @@
         band_out[:, m * half : (m + 1) * half] = turn_ref[pl.ds(pl.multiple_of(position, 8), piece_count), :]
 
 
-def gather_kernel(half, devices, cols, takes, band_ref, eig_ref, all_ref, above_ref, under_ref, rev_ref, sems):
-    z_send, z_recv, p_send, p_recv, c_send, c_recv, e_send, e_recv, own_sem = sems
-    d, c = lax.axis_index("band"), lax.axis_index("cols")
-    count = band_ref.shape[0]
-    full = half // count
-    pieces = full + 1
-    chips = devices // 2
-    tall = chips // 2
-    chip, core = d // 2, d % 2
-    partner = chip * 2 + 1 - core
-    spot = (1 - chip % 2) * (chip // 2) + (chip % 2) * (chips - 1 - chip // 2)
-
-    def at(rel):
-        ring = (spot + rel + chips) % chips
-        turn = ring // tall
-        return ((1 - turn) * 2 * ring + turn * (2 * (chips - 1 - ring) + 1)) * 2 + core
-
-    for r in range(count):
-        rev_ref[r : r + 1, :] = band_ref[count - 1 - r : count - r, :]
-
-    barrier = pltpu.get_barrier_semaphore()
-    peers = [(at(1), c), (at(-1), c), (partner, c)]
-    for hop in range(1, len(takes) + 1):
-        peers += [((d + hop) % devices, c), ((d - hop + devices) % devices, c)]
-    for peer in peers:
-        pl.semaphore_signal(barrier, inc=1, device_id=peer, device_id_type=pl.DeviceIdType.MESH)
-
-    @pl.when(c > 0)
-    def _():
-        pl.semaphore_signal(barrier, inc=1, device_id=(d, c - 1), device_id_type=pl.DeviceIdType.MESH)
-
-    @pl.when(c < cols - 1)
-    def _():
-        pl.semaphore_signal(barrier, inc=1, device_id=(d, c + 1), device_id_type=pl.DeviceIdType.MESH)
-
-    beside = (c + cols - 1) // cols + 1 - (c + 1) // cols
-    pl.semaphore_wait(barrier, len(peers) + beside)
-
-    def send(src, dst, send_sem, recv_sem, device):
-        return pltpu.make_async_remote_copy(
-            src_ref=src,
-            dst_ref=dst,
-            send_sem=send_sem,
-            recv_sem=recv_sem,
-            device_id=device,
-            device_id_type=pl.DeviceIdType.MESH,
-        )
-
-    def rows_of(p, part):
-        first, size = (half - (p + 1) * count, count) if p < full else (half, 8)
-        if part is not None and p < full:
-            first, size = first + part * (size // 2), size // 2
-        return pl.ds(first, size)
-
-    def place(dev, p, part=None):
-        return all_ref.at[dev, rows_of(p, part)]
-
-    def source(p):
-        return rev_ref if p < full else band_ref.at[pl.ds(0, 8)]
-
-    def along(p, up, src):
-        to = (c + 1) % cols if up else (c - 1 + cols) % cols
-        return send(src, place(d, p), z_send.at[p, int(up)], z_recv.at[p], (d, to))
-
-    def hops(p):
-        for j in range(1, chips // 2 + 1):
-            for way in (1, -1):
-                if 2 * j < chips:
-                    yield j, way, None
-                elif p < full:
-                    yield j, way, 0 if way == 1 else 1
-                elif way == 1:
-                    yield j, way, None
-
-    def across(p, j, way, part, src=None):
-        dev = at(-way * (j - 1))
-        src = place(dev, p, part) if src is None else src
-        which = 2 * j + (way + 1) // 2
-        return send(src, place(dev, p, part), p_send.at[p, which], p_recv.at[p, which], (at(way), c))
-
-    def pair(p, j, way, part, src=None):
-        dev = at(-way * j)
-        src = place(dev, p, part) if src is None else src
-        which = 2 * j + (way + 1) // 2
-        return send(src, place(dev, p, part), c_send.at[p, which], c_recv.at[p, which], (partner, c))
-
-    def own(p):
-        return pltpu.make_async_copy(source(p), place(d, p), own_sem)
-
-    def first_hops(p, src):
-        for j, way, part in hops(p):
-            if j == 1:
-                across(p, 1, way, part, src).start()
-        pair(p, 0, 1, None, src).start()
-
-    rows_dev = eig_ref.shape[0]
-    halos = []
-    end = sum(takes)
-    for hop, take in enumerate(takes, 1):
-        halos.append(
-            send(
-                eig_ref.at[pl.ds(rows_dev - take, take)],
-                above_ref.at[pl.ds(end - take, take)],
-                e_send.at[hop],
-                e_recv.at[hop],
-                ((d + hop) % devices, c),
-            )
-        )
-        end -= take
-    halos.append(
-        send(eig_ref.at[pl.ds(0, 8)], under_ref, e_send.at[0], e_recv.at[0], ((d - 1 + devices) % devices, c))
-    )
-
-    for p in range(pieces):
-
-        @pl.when(c == p)
-        def _():
-            @pl.when(c < cols - 1)
-            def _():
-                along(p, True, source(p)).start()
-
-            @pl.when(c > 0)
-            def _():
-                along(p, False, source(p)).start()
-
-            first_hops(p, source(p))
-            own(p).start()
-
-    def receive(p):
-        @pl.when(c != p)
-        def _():
-            along(p, True, place(d, p)).wait_recv()
-
-            @pl.when((c > p) & (c < cols - 1))
-            def _():
-                along(p, True, place(d, p)).start()
-
-            @pl.when((c < p) & (c > 0))
-            def _():
-                along(p, False, place(d, p)).start()
-
-            first_hops(p, place(d, p))
-
-    def relay(p, level):
-        for j, way, part in hops(p):
-            if j == level:
-                across(p, j, way, part).wait_recv()
-                for j2, way2, part2 in hops(p):
-                    if j2 == j + 1 and way2 == way:
-                        across(p, j2, way, part2).start()
-                pair(p, j, way, part).start()
-
-    for p in reversed(range(pieces)):
-        receive(p)
-    for halo in halos:
-        halo.start()
-    for level in range(1, chips // 2 + 1):
-        for p in reversed(range(pieces)):
-            relay(p, level)
-    for p in range(pieces):
-
-        @pl.when(c == p)
-        def _():
-            own(p).wait()
-
-        @pl.when((c >= p) & (c < cols - 1))
-        def _():
-            along(p, True, place(d, p)).wait_send()
-
-        @pl.when((c <= p) & (c > 0))
-        def _():
-            along(p, False, place(d, p)).wait_send()
-
-        for j, way, part in hops(p):
-            across(p, j, way, part).wait_send()
-            pair(p, j, way, part).wait()
-        pair(p, 0, 1, None).wait()
-    for halo in halos:
-        halo.wait()
-
-
 def body(band_diagonals, eigenvectors):
     piece_count, rows_dev = band_diagonals.shape
     cols = lax.axis_size("cols")
@@ -489,36 +478,27 @@
         takes.append(min(halo * half - sum(takes), rows_dev))
     pieces = half // piece_count + 1
     dma = pltpu.SemaphoreType.DMA
-    band, above, under = pl.pallas_call(
-        functools.partial(gather_kernel, half, devices, cols, takes),
-        out_shape=(
-            jax.ShapeDtypeStruct((devices, half + 8, rows_dev), f32),
-            jax.ShapeDtypeStruct((halo * half, columns), f32),
-            jax.ShapeDtypeStruct((8, columns), f32),
-        ),
-        in_specs=[vmem] * 2,
-        out_specs=(vmem,) * 3,
-        scratch_shapes=[
-            pltpu.VMEM((piece_count, rows_dev), f32),
-            [
-                dma((pieces, 2)),
-                dma((pieces,)),
-                dma((pieces, devices + 2)),
-                dma((pieces, devices + 2)),
-                dma((pieces, devices + 2)),
-                dma((pieces, devices + 2)),
-                dma((len(takes) + 1,)),
-                dma((len(takes) + 1,)),
-                dma,
-            ]
-        ],
-        compiler_params=pltpu.CompilerParams(collective_id=0, has_side_effects=True),
-    )(band_diagonals, eigenvectors)
-
     slots = blocks + 4
     pair_count = sweeps * (sweeps - 1) // 2 + 1
     scratch = (
-        [pltpu.VMEM((slots, half, half), f32)] * 3
+        [
+            pltpu.VMEM((blocks, half + 8, half), f32),
+            pltpu.VMEM((halo * half, columns), f32),
+            pltpu.VMEM((8, columns), f32),
+            pltpu.VMEM((blocks_dev, piece_count, half), f32),
+            [
+                dma((blocks_dev, cols)),
+                dma((pieces, blocks_dev)),
+                dma((blocks_dev,)),
+                dma((devices // 2, blocks_dev)),
+                dma((devices // 2, blocks_dev)),
+                dma((devices // 2, blocks_dev)),
+                dma((devices // 2, blocks_dev)),
+                dma((len(takes) + 1,)),
+                dma((len(takes) + 1,)),
+            ],
+        ]
+        + [pltpu.VMEM((slots, half, half), f32)] * 3
         + [
             pltpu.VMEM((half, half), f32),
             pltpu.VMEM((8, half), f32),
@@ -529,16 +509,18 @@
         + [pltpu.VMEM((slots, 8, half), f32)] * pair_count
     )
     return pl.pallas_call(
-        functools.partial(chase_kernel, blocks, half, blocks_dev, halo, piece_count, sweeps),
+        functools.partial(kernel, half, devices, cols, takes, blocks, halo, sweeps),
         out_shape=(
             jax.ShapeDtypeStruct((piece_count, rows_dev), f32),
             jax.ShapeDtypeStruct((rows_dev, columns), f32),
         ),
-        in_specs=[vmem] * 4,
+        in_specs=[vmem] * 2,
         out_specs=(vmem, vmem),
         scratch_shapes=scratch,
-        compiler_params=pltpu.CompilerParams(vmem_limit_bytes=62 * 1024 * 1024),
-    )(band, above, eigenvectors, under)
+        compiler_params=pltpu.CompilerParams(
+            collective_id=0, has_side_effects=True, vmem_limit_bytes=62 * 1024 * 1024
+        ),
+    )(band_diagonals, eigenvectors)
 
 
 def solution(mesh):

time: 42 us -> 38.2 us (0.910)
  the two profiles are of different devices: /device:TPU:25 before, /device:TPU:5 now
where the time goes in v4:
time: 38.2 us; the launch traced here: 38 us
  Pallas kernels  35.1 us (92%)
  local copies, waits for them, and re-layouts  2.26 us (6%)
  between operations  0.65 us (2%)
    pallas_call x1, Pallas kernels, body(): pl.pallas_call(functools.partial(kernel, half, devices, cols, takes, bloc...  35.1 us
    unnamed x4, local copies, waits for them, and re-layouts  2.26 us

profile of v4, /device:TPU:5, one launch (start us, length us, event | category | flops | bytes accessed | tf_op | source)
XLA Modules:
  0.0 38.0 jit_solution(8470588278989504268)
XLA Ops:
  0.6 35.1 %shard_map.41 = (f32[64,384]{1,0:T(8,128)}, f32[384,128]{1,0:T(8,128)}) custom-call(f32[64,384]{1,0:T(8,128)} %band_in.1, f32[384,128]{1,0:T(8,128)} %eig_ref.1), custom_call_target="tpu_custom_call" | custom-call | tf_op jit(solution)/shard_map/pallas_call | solution.py:511
  35.7 0.0 copy-start
  35.8 1.6 %copy.6 = f32[64,384]{1,0:T(8,128)} copy(f32[64,384]{1,0:T(8,128)} %get-tuple-element.4) | data formatting | bytes 196608
  37.3 0.0 copy-done
  37.3 0.7 %copy.7 = f32[384,128]{1,0:T(8,128)} copy(f32[384,128]{1,0:T(8,128)S(1)} %copy-done) | data formatting | bytes 393216
Async XLA Ops:
  35.7 1.6 %copy-start = (f32[384,128]{1,0:T(8,128)S(1)}, f32[384,128]{1,0:T(8,128)}, u32[]{:S(2)}) copy-start(f32[384,128]{1,0:T(8,128)} %get-tuple-element.5) | copy-start | bytes 589828

commit v5 on v4

--- a/solution.py
+++ b/solution.py
@@ -14,16 +14,17 @@
 UNROLL = 2
 
 
-def kernel(half, devices, cols, takes, blocks, halo, sweeps, band_in, eig_ref, band_out, eig_out, *refs):
-    all_ref, above_ref, under_ref, rev_ref, sems = refs[:5]
-    refs = refs[5:]
-    d_ref, l_ref, t_ref, eye_ref, edge_ref, raw_ref, turn_ref = refs[:7]
-    v_refs = refs[7 : 7 + sweeps]
-    tau_refs = refs[7 + sweeps : 7 + 2 * sweeps]
+def kernel(half, devices, cols, takes, blocks, halo, sweeps, band_ref, eig_ref, *refs):
+    field_out, v_out, tau_out, above_ref, under_ref = refs[:5]
+    all_ref, band_in, rev_ref, in_sem, sems = refs[5:10]
+    refs = refs[10:]
+    d_ref, l_ref, t_ref, eye_ref, raw_ref = refs[:5]
+    v_refs = refs[5 : 5 + sweeps]
+    tau_refs = refs[5 + sweeps : 5 + 2 * sweeps]
     last = sweeps - 1
     pairs = [(a, b) for b in range(1, sweeps) for a in range(b)] + [(last, last)]
-    fields = dict(zip(pairs, refs[7 + 2 * sweeps :]))
-    piece_count, blocks_dev = band_in.shape[0], band_in.shape[1] // half
+    fields = dict(zip(pairs, refs[5 + 2 * sweeps :]))
+    blocks_dev = band_ref.shape[1] // half
     steps = blocks - 2
     row = lax.broadcasted_iota(jnp.int32, (half, half), 0)
     col = lax.broadcasted_iota(jnp.int32, (half, half), 1)
@@ -35,7 +36,7 @@
 
     z_send, z_recv, own_sem, x_send, x_recv, p_send, p_recv, e_send, e_recv = sems
     d, c = lax.axis_index("band"), lax.axis_index("cols")
-    deep, rows_dev = band_in.shape
+    deep, rows_dev = band_ref.shape
     full = half // deep
     pieces = full + 1
     parts = rows_dev // half
@@ -43,6 +44,8 @@
     chip, core = d // 2, d % 2
     partner = chip * 2 + 1 - core
 
+    inward = pltpu.make_async_copy(band_ref, band_in, in_sem)
+    inward.start()
     barrier = pltpu.get_barrier_semaphore()
     peers = [(d, (c + hop) % cols) for hop in range(1, cols)]
     peers += [((chip + hop) % chips * 2 + core, c) for hop in range(1, chips)]
@@ -52,18 +55,19 @@
     for peer in peers:
         pl.semaphore_signal(barrier, inc=1, device_id=peer, device_id_type=pl.DeviceIdType.MESH)
 
-    for r in range(deep):
-        for m in range(parts):
-            rev_ref[m, r : r + 1, :] = band_in[deep - 1 - r : deep - r, m * half : (m + 1) * half]
-
     for spot in (0, 1, blocks + 2):
         d_ref[spot] = zero
     for spot in (0, blocks + 1):
         l_ref[spot] = zero
         t_ref[spot] = zero
-    for ref in v_refs + tau_refs + tuple(fields.values()) + (raw_ref, edge_ref):
+    for ref in v_refs + tau_refs + tuple(fields.values()) + (raw_ref,):
         ref[...] = jnp.zeros(ref.shape, jnp.float32)
     eye_ref[...] = jnp.where(eye, 1.0, 0.0)
+
+    inward.wait()
+    for r in range(deep):
+        for m in range(parts):
+            rev_ref[m, r : r + 1, :] = band_in[deep - 1 - r : deep - r, m * half : (m + 1) * half]
 
     pl.semaphore_wait(barrier, len(peers))
 
@@ -217,16 +221,9 @@
         return jnp.broadcast_to(line, (8, half))
 
     def begin(s):
-        base = wide(d_ref[2, s : s + 1, :])
-        x = jnp.where(col8 > s, base, wide(t_ref[2, s : s + 1, :]))
-        diagonal = base
+        x = jnp.where(col8 > s, wide(d_ref[2, s : s + 1, :]), wide(t_ref[2, s : s + 1, :]))
         for a in range(s):
-            raw = raw_ref[a]
-            x = x - rows_sum(fields[a, s][2] * at_lane(raw, s))
-            diagonal = diagonal - 2.0 * raw[0:1, :] * raw[4:5, :]
-        length = norms(x, s + 1)[2]
-        edge = jnp.where((row8 == s) & (col8 == s), diagonal, edge_ref[...])
-        edge_ref[...] = jnp.where((row8 == s + 1) & (col8 == s), -length, edge)
+            x = x - rows_sum(fields[a, s][2] * at_lane(raw_ref[a], s))
         return (x,) + (jnp.zeros((8, half), jnp.float32),) * 4
 
     def targets(s):
@@ -370,17 +367,34 @@
     for copy in halos:
         copy.wait()
 
+    first = d * parts
+    for s in range(sweeps):
+        for e in range(halo + parts):
+            spot = jnp.clip(first - halo + e, -1, blocks - 1) + 1
+            v_out[s, e : e + 1, :] = v_refs[s][spot, 0:1, :]
+            tau_out[s, e : e + 1, :] = tau_refs[s][spot, 0:1, :]
+        for n in range(parts + 2):
+            field_out[s, n] = fields[s, last][first + n]
+
+
+def finish_kernel(half, blocks, halo, sweeps, *refs):
+    band_ref, eig_ref, field_ref, v_ref, tau_ref, above_ref, under_ref, band_out, eig_out, turn_ref = refs
+    piece_count, blocks_dev = band_ref.shape[0], band_ref.shape[1] // half
+    steps = blocks - 2
+    row = lax.broadcasted_iota(jnp.int32, (half, half), 0)
+    col = lax.broadcasted_iota(jnp.int32, (half, half), 1)
+    eye = row == col
+    row8 = lax.broadcasted_iota(jnp.int32, (8, half), 0)
     device = lax.axis_index("band")
-    base = device * blocks_dev - halo
+    first = device * blocks_dev
     eig = [above_ref[e * half : (e + 1) * half, :] for e in range(halo)]
     eig += [eig_ref[e * half : (e + 1) * half, :] for e in range(blocks_dev)]
     eig.append(under_ref[...])
     for s in reversed(range(sweeps)):
         lead_rows = s + 1
         for e in range(sweeps - 1 - s + halo - sweeps, halo + blocks_dev):
-            spot = jnp.clip(base + e, -1, blocks - 1) + 1
-            v = jnp.sum(v_refs[s][spot, 0:1, :] * eye_ref[...], axis=1, keepdims=True)
-            tau = tau_refs[s][spot, 0:1, :]
+            v = jnp.sum(jnp.where(eye, v_ref[s, e : e + 1, :], 0.0), axis=1, keepdims=True)
+            tau = tau_ref[s, e : e + 1, :]
             low, high = eig[e], eig[e + 1]
             mixed = jnp.concatenate([jnp.where(row8 < lead_rows, high[:8], low[:8]), low[8:]], 0)
             inner = tau * jnp.sum(v * mixed, axis=0, keepdims=True)
@@ -397,40 +411,25 @@
             precision=lax.Precision.HIGHEST, preferred_element_type=jnp.float32,
         )
 
-    def stack(k, shift=0, drop=None):
+    def stack(n, shift=0, drop=None):
         parts = []
         for a in range(sweeps):
-            part = fields[a, last][k + 2]
+            part = field_ref[a, n]
             part = part if drop is None else jnp.where(row8 == drop, 0.0, part)
             parts.append(pltpu.roll(part, shift, 0) if shift else part)
         return jnp.concatenate(parts, 0)
 
-    def final_d(k):
-        outer = jnp.where(col > last, d_ref[k + 2], t_ref[k + 2])
-        inner = jnp.where(col > last, l_ref[k + 2], d_ref[k + 3])
-        return jnp.where(row > last, outer, inner) - product(stack(k), stack(k, 4))
-
-    def final_l(k):
-        outer = jnp.where(col > last, l_ref[k + 2], d_ref[k + 3])
-        inner = jnp.where(col > last, 0.0, l_ref[k + 3])
-        block = jnp.where(row > last, outer, inner) - product(stack(k + 1, 0, 2), stack(k, 1))
-        cleared = jnp.where(k <= steps - 2, sweeps, -1)
-        return jnp.where((col == cleared) & (row != sweeps), 0.0, block)
-
-    edge = jnp.concatenate([edge_ref[...], zero[8:]], axis=0)
     bottom, lead = [], []
-    for a in range(last):
-        bottom.append(jnp.where(row8 == 1, fields[a, last][steps + 2], 0.0))
-        lead.append(pltpu.roll(jnp.where(row8 == 3, fields[a, last][steps], 0.0), 6, 0))
+    for a in range(sweeps - 1):
+        bottom.append(jnp.where(row8 == 1, field_ref[a, blocks_dev], 0.0))
+        lead.append(pltpu.roll(jnp.where(row8 == 3, field_ref[a, blocks_dev - 2], 0.0), 6, 0))
     rest = -product(jnp.concatenate(bottom, 0), jnp.concatenate(lead, 0))
     flip = jnp.where((row + col == half) | ((row == 0) & (col == 0)), 1.0, 0.0)
     position = lax.axis_index("cols") * piece_count
-    first = device * blocks_dev
-    d_last = [final_d(first + m - 1) for m in range(blocks_dev + 1)]
-    l_last = [final_l(first + m - 2) for m in range(blocks_dev + 1)]
-    top = jnp.where(device == 0, half, 0)
-    d_last[0] = jnp.where(row < top, jnp.where(row < sweeps, edge, 0.0), d_last[0])
-    l_last[1] = jnp.where(row < top, jnp.where(row >= sweeps, edge, 0.0), l_last[1])
+    d_last = [-product(stack(m + 1), stack(m + 1, 4)) for m in range(blocks_dev + 1)]
+    l_last = [-product(stack(m + 1, 0, 2), stack(m, 1)) for m in range(blocks_dev + 1)]
+    diagonal = position + lax.broadcasted_iota(jnp.int32, (piece_count, half), 0)
+    across = lax.broadcasted_iota(jnp.int32, (piece_count, half), 1)
     for m in range(blocks_dev):
         b = first + m
         lim = jnp.where(b > 0, half, 0)
@@ -456,7 +455,12 @@
             turned = jnp.dot(part, flip, precision=lax.Precision.HIGHEST)
             turned = pltpu.roll(turned, 0, 1, stride=1, stride_axis=0)
             turn_ref[n * half : (n + 1) * half, :] = turned.T
-        band_out[:, m * half : (m + 1) * half] = turn_ref[pl.ds(pl.multiple_of(position, 8), piece_count), :]
+        turned = turn_ref[pl.ds(pl.multiple_of(position, 8), piece_count), :]
+        place = b * half + across - diagonal
+        cleared = (place & (half - 1) == sweeps) & (diagonal > half) & (place < (steps - 1) * half)
+        cleared = cleared | ((place < sweeps) & (diagonal >= 2))
+        span = slice(m * half, (m + 1) * half)
+        band_out[:, span] = jnp.where(cleared, 0.0, band_ref[:, span] + turned)
 
 
 def body(band_diagonals, eigenvectors):
@@ -483,9 +487,9 @@
     scratch = (
         [
             pltpu.VMEM((blocks, half + 8, half), f32),
-            pltpu.VMEM((halo * half, columns), f32),
-            pltpu.VMEM((8, columns), f32),
+            pltpu.VMEM((piece_count, rows_dev), f32),
             pltpu.VMEM((blocks_dev, piece_count, half), f32),
+            dma,
             [
                 dma((blocks_dev, cols)),
                 dma((pieces, blocks_dev)),
@@ -501,26 +505,39 @@
         + [pltpu.VMEM((slots, half, half), f32)] * 3
         + [
             pltpu.VMEM((half, half), f32),
-            pltpu.VMEM((8, half), f32),
             pltpu.VMEM((sweeps, 8, half), f32),
-            pltpu.VMEM((double, half), f32),
         ]
         + [pltpu.VMEM((blocks + 1, 8, half), f32)] * (2 * sweeps)
         + [pltpu.VMEM((slots, 8, half), f32)] * pair_count
     )
-    return pl.pallas_call(
+    anywhere = pl.BlockSpec(memory_space=pl.ANY)
+    lines = -(-(halo + blocks_dev) // 8) * 8
+    fields, v, tau, above, under = pl.pallas_call(
         functools.partial(kernel, half, devices, cols, takes, blocks, halo, sweeps),
         out_shape=(
-            jax.ShapeDtypeStruct((piece_count, rows_dev), f32),
-            jax.ShapeDtypeStruct((rows_dev, columns), f32),
+            jax.ShapeDtypeStruct((sweeps, blocks_dev + 2, 8, half), f32),
+            jax.ShapeDtypeStruct((sweeps, lines, half), f32),
+            jax.ShapeDtypeStruct((sweeps, lines, half), f32),
+            jax.ShapeDtypeStruct((halo * half, columns), f32),
+            jax.ShapeDtypeStruct((8, columns), f32),
         ),
-        in_specs=[vmem] * 2,
-        out_specs=(vmem, vmem),
+        in_specs=[anywhere] * 2,
+        out_specs=(vmem,) * 3 + (anywhere,) * 2,
         scratch_shapes=scratch,
         compiler_params=pltpu.CompilerParams(
             collective_id=0, has_side_effects=True, vmem_limit_bytes=62 * 1024 * 1024
         ),
     )(band_diagonals, eigenvectors)
+    return pl.pallas_call(
+        functools.partial(finish_kernel, half, blocks, halo, sweeps),
+        out_shape=(
+            jax.ShapeDtypeStruct((piece_count, rows_dev), f32),
+            jax.ShapeDtypeStruct((rows_dev, columns), f32),
+        ),
+        in_specs=[vmem] * 7,
+        out_specs=(vmem, vmem),
+        scratch_shapes=[pltpu.VMEM((double, half), f32)],
+    )(band_diagonals, eigenvectors, fields, v, tau, above, under)
 
 
 def solution(mesh):

time: 38.2 us -> 36.9 us (0.966)
  local copies, waits for them, and re-layouts: 2.26 us -> 0 us
  Pallas kernels: 35.1 us -> 36.1 us
    pallas_call x0 -> x1, Pallas kernels: none -> 3.21 us  [body(): pl.pallas_call(functools.partial(finish_kernel, half, blocks, halo, sweep...]
    unnamed x4 -> x0, local copies, waits for them, and re-layouts: 2.26 us -> none
    pallas_call x1, Pallas kernels: 35.1 us -> 32.9 us  [body(): pl.pallas_call(functools.partial(kernel, half, devices, cols, takes, bloc...]
where the time goes in v5:
time: 36.9 us; the launch traced here: 36.7 us
  Pallas kernels  36.1 us (98%)
  between operations  0.64 us (2%)
    pallas_call x1, Pallas kernels, body(): pl.pallas_call(functools.partial(kernel, half, devices, cols, takes, bloc...  32.9 us
    pallas_call x1, Pallas kernels, body(): pl.pallas_call(functools.partial(finish_kernel, half, blocks, halo, sweep...  3.21 us

profile of v5, /device:TPU:5, one launch (start us, length us, event | category | flops | bytes accessed | tf_op | source)
XLA Modules:
  0.0 36.7 jit_solution(387461888120656369)
XLA Ops:
  0.6 32.9 %shard_map.41 = (f32[4,5,8,128]{3,2,1,0:T(8,128)}, f32[4,8,128]{2,1,0:T(8,128)}, f32[4,8,128]{2,1,0:T(8,128)}, f32[512,128]{1,0:T(8,128)}, f32[8,128]{1,0:T(8,128)}) custom-call(f32[64,384]{1,0:T(8,128)} %refs_0_.1, f32[384,128]{1,0:T(8,128)} %refs_1_.1), custom_call_target="tpu_custom_call" | custom-call | tf_op jit(solution)/shard_map/pallas_call | solution.py:515
  33.5 3.2 %shard_map.42 = (f32[64,384]{1,0:T(8,128)}, f32[384,128]{1,0:T(8,128)}) custom-call(f32[64,384]{1,0:T(8,128)} %refs_0_.1, f32[384,128]{1,0:T(8,128)} %refs_1_.1, f32[4,5,8,128]{3,2,1,0:T(8,128)} %get-tuple-element.7.refs_2_, f32[4,8,128]{2,1,0:T(8,128)} %get-tuple-element.8.refs_3_, f32[4,8,128]{2,1,0:T(8,128)} %get-tuple-element.9.refs_4_, ...), custom_call_target="tpu_custom_call" | custom-call | tf_op jit(solution)/shard_map/pallas_call | solution.py:531

commit v6 on v5

--- a/solution.py
+++ b/solution.py
@@ -11,7 +11,7 @@
 LAG = 3
 AHEAD = 4
 EARLY = 3
-UNROLL = 2
+GROUP = 3
 
 
 def kernel(half, devices, cols, takes, blocks, halo, sweeps, band_ref, eig_ref, *refs):
@@ -167,7 +167,10 @@
     def duty(block):
         owner, side, m = sides(block)
 
-        @pl.when((side == core) & (owner != chip) & (block < blocks))
+        if block >= blocks:
+            return
+
+        @pl.when((core == side) & (chip != owner))
         def _():
             arrived(owner, m).wait_recv()
             share(owner, m).start()
@@ -175,7 +178,10 @@
     def need(block):
         owner, side, m = sides(block)
 
-        @pl.when((side != core) & (block < blocks))
+        if block >= blocks:
+            return
+
+        @pl.when(core != side)
         def _():
             share(owner, m).wait_recv()
 
@@ -237,8 +243,8 @@
             ref[k + 2, 4:5, :] = jnp.where(other, wide(ref[k + 2, 4:5, :]), inside)[0:1]
             if b > s:
                 ref[k + 1, 7:8, :] = jnp.where(other, inside, wide(ref[k + 1, 7:8, :]))[0:1]
-        if s < last:
-            raw_ref[s, 0:1, :] = jnp.where(col8 < jnp.where(k == 0, half, 0), inside, wide(raw_ref[s, 0:1, :]))[0:1]
+        if s < last and k == 0:
+            raw_ref[s, 0:1, :] = inside[0:1]
 
     def chain(s, k, x, hung, inside_past, v_past, tau_past):
         new = s + 1
@@ -302,33 +308,27 @@
                 ref[k + 2, 4:5, :] = beneath[0:1]
                 ref[k + 1, 3:4, :] = jnp.where(other, v, 0.0)[0:1]
                 ref[k, 2:3, :] = jnp.where(other, across, 0.0)[0:1]
-        if s < last:
-            raw_ref[s, 3:4, :] = jnp.where(col8 < jnp.where(k == 1, half, 0), across, wide(raw_ref[s, 3:4, :]))[0:1]
-            raw_ref[s, 4:5, :] = jnp.where(col8 < jnp.where(k == 0, half, 0), v, wide(raw_ref[s, 4:5, :]))[0:1]
+        if s < last and k == 1:
+            raw_ref[s, 3:4, :] = across[0:1]
+        if s < last and k == 0:
+            raw_ref[s, 4:5, :] = v[0:1]
         return x_next, beneath, inside, v, tau
 
     def phase(start, stop, chains, states):
         def wave(t, states):
             done = {s: chain(s, t - LAG * s, *state) for s, state in reversed(list(zip(chains, states)))}
-            if start < steps:
-                unpack(jnp.minimum(t + AHEAD, blocks - 1))
+            if t + AHEAD < blocks:
+                unpack(t + AHEAD)
             return tuple(done[s] for s in chains)
 
-        def turn(t, states, size):
-            if start < steps:
-                for more in range(size):
-                    duty(t + more + AHEAD + EARLY)
-                for more in range(size):
-                    need(t + more + AHEAD)
-            for more in range(size):
-                states = wave(t + more, states)
-            return states
-
-        size = min(UNROLL, stop - start)
-        turns = (stop - start) // size
-        states = lax.fori_loop(0, turns, lambda i, st: turn(start + i * size, st, size), tuple(states))
-        if start + turns * size < stop:
-            states = turn(start + turns * size, states, stop - start - turns * size)
+        for begun in range(start, stop, GROUP):
+            waves = range(begun, min(begun + GROUP, stop))
+            for t in waves:
+                duty(t + AHEAD + EARLY)
+            for t in waves:
+                need(t + AHEAD)
+            for t in waves:
+                states = wave(t, states)
         return states
 
     def drain(s, state):

time: 36.9 us -> 35.3 us (0.957)
  Pallas kernels: 36.1 us -> 34.5 us
    pallas_call x1, Pallas kernels: 32.9 us -> 31.3 us  [body(): pl.pallas_call(functools.partial(kernel, half, devices, cols, takes, bloc...]
where the time goes in v6:
time: 35.3 us; the launch traced here: 35.1 us
  Pallas kernels  34.5 us (98%)
  between operations  0.64 us (2%)
    pallas_call x1, Pallas kernels, body(): pl.pallas_call(functools.partial(kernel, half, devices, cols, takes, bloc...  31.3 us
    pallas_call x1, Pallas kernels, body(): pl.pallas_call(functools.partial(finish_kernel, half, blocks, halo, sweep...  3.21 us

profile of v6, /device:TPU:5, one launch (start us, length us, event | category | flops | bytes accessed | tf_op | source)
XLA Modules:
  0.0 35.1 jit_solution(17524945423666021594)
XLA Ops:
  0.6 31.3 %shard_map.41 = (f32[4,5,8,128]{3,2,1,0:T(8,128)}, f32[4,8,128]{2,1,0:T(8,128)}, f32[4,8,128]{2,1,0:T(8,128)}, f32[512,128]{1,0:T(8,128)}, f32[8,128]{1,0:T(8,128)}) custom-call(f32[64,384]{1,0:T(8,128)} %refs_0_.1, f32[384,128]{1,0:T(8,128)} %refs_1_.1), custom_call_target="tpu_custom_call" | custom-call | tf_op jit(solution)/shard_map/pallas_call | solution.py:515
  31.9 3.2 %shard_map.42 = (f32[64,384]{1,0:T(8,128)}, f32[384,128]{1,0:T(8,128)}) custom-call(f32[64,384]{1,0:T(8,128)} %refs_0_.1, f32[384,128]{1,0:T(8,128)} %refs_1_.1, f32[4,5,8,128]{3,2,1,0:T(8,128)} %get-tuple-element.7.refs_2_, f32[4,8,128]{2,1,0:T(8,128)} %get-tuple-element.8.refs_3_, f32[4,8,128]{2,1,0:T(8,128)} %get-tuple-element.9.refs_4_, ...), custom_call_target="tpu_custom_call" | custom-call | tf_op jit(solution)/shard_map/pallas_call | solution.py:531

commit v7 on v6

--- a/solution.py
+++ b/solution.py
@@ -99,13 +99,21 @@
     def chunk(owner, m):
         return all_ref.at[owner * parts + m]
 
-    def across(to, m):
-        src = chunk(d, m)
-        return send(src, src, x_send.at[to, m], x_recv.at[chip, m], (to * 2 + core, c))
-
-    def arrived(owner, m):
-        src = chunk(owner * 2 + core, m)
-        return send(src, src, x_send.at[owner, m], x_recv.at[owner, m], (owner * 2 + core, c))
+    def across(to, m, p, src=None):
+        dst = place(p, m)
+        src = dst if src is None else src
+        return send(src, dst, x_send.at[to, m, p], x_recv.at[chip, m, p], (to * 2 + core, c))
+
+    def arrived(owner, m, p):
+        dst = all_ref.at[(owner * 2 + core) * parts + m, rows_of(p)]
+        return send(dst, dst, x_send.at[owner, m, p], x_recv.at[owner, m, p], (owner * 2 + core, c))
+
+    def spread(m, p, src=None):
+        for to in reversed(range(chips)):
+
+            @pl.when(chip != to)
+            def _():
+                across(to, m, p, src).start()
 
     def share(owner, m):
         src = chunk(owner * 2 + core, m)
@@ -137,12 +145,13 @@
                     if to != p:
                         along(p, m, to).start()
                 own(p, m).start()
+                spread(m, p, source(p, m))
 
     for copy in halos:
         copy.start()
 
     for m in range(parts):
-        for p in range(pieces):
+        for p in reversed(range(pieces)):
 
             @pl.when(c == p)
             def _():
@@ -151,12 +160,7 @@
             @pl.when(c != p)
             def _():
                 along(p, m, c).wait_recv()
-
-        for to in reversed(range(chips)):
-
-            @pl.when(chip != to)
-            def _():
-                across(to, m).start()
+                spread(m, p)
 
         share(chip, m).start()
 
@@ -172,7 +176,8 @@
 
         @pl.when((core == side) & (chip != owner))
         def _():
-            arrived(owner, m).wait_recv()
+            for p in range(pieces):
+                arrived(owner, m, p).wait_recv()
             share(owner, m).start()
 
     def need(block):
@@ -361,7 +366,8 @@
 
             @pl.when(chip != owner)
             def _():
-                across(owner, m).wait_send()
+                for p in range(pieces):
+                    across(owner, m, p).wait_send()
 
             share(owner, m).wait_send()
     for copy in halos:
@@ -451,11 +457,10 @@
         c2 = jnp.where(row < lim, c2, 0.0)
         lower = jnp.where(col <= row, c0, c1)
         upper = jnp.where(col <= row, c1, c2)
-        for n, part in enumerate((lower, upper)):
-            turned = jnp.dot(part, flip, precision=lax.Precision.HIGHEST)
-            turned = pltpu.roll(turned, 0, 1, stride=1, stride_axis=0)
-            turn_ref[n * half : (n + 1) * half, :] = turned.T
-        turned = turn_ref[pl.ds(pl.multiple_of(position, 8), piece_count), :]
+        part = jnp.where(row < jnp.where(position < half, half, 0), lower, upper)
+        turned = jnp.dot(part, flip, precision=lax.Precision.HIGHEST)
+        turn_ref[m] = pltpu.roll(turned, 0, 1, stride=1, stride_axis=0).T
+        turned = turn_ref[m, pl.ds(pl.multiple_of(position % half, 8), piece_count), :]
         place = b * half + across - diagonal
         cleared = (place & (half - 1) == sweeps) & (diagonal > half) & (place < (steps - 1) * half)
         cleared = cleared | ((place < sweeps) & (diagonal >= 2))
@@ -494,8 +499,8 @@
                 dma((blocks_dev, cols)),
                 dma((pieces, blocks_dev)),
                 dma((blocks_dev,)),
-                dma((devices // 2, blocks_dev)),
-                dma((devices // 2, blocks_dev)),
+                dma((devices // 2, blocks_dev, pieces)),
+                dma((devices // 2, blocks_dev, pieces)),
                 dma((devices // 2, blocks_dev)),
                 dma((devices // 2, blocks_dev)),
                 dma((len(takes) + 1,)),
@@ -536,7 +541,7 @@
         ),
         in_specs=[vmem] * 7,
         out_specs=(vmem, vmem),
-        scratch_shapes=[pltpu.VMEM((double, half), f32)],
+        scratch_shapes=[pltpu.VMEM((blocks_dev, half, half), f32)],
     )(band_diagonals, eigenvectors, fields, v, tau, above, under)
 
 

time: 35.3 us -> 34.4 us (0.975)
  the two profiles are of different devices: /device:TPU:5 before, /device:TPU:23 now
where the time goes in v7:
time: 34.4 us; the launch traced here: 34.2 us
  Pallas kernels  33.6 us (98%)
  between operations  0.64 us (2%)
    pallas_call x1, Pallas kernels, body(): pl.pallas_call(functools.partial(kernel, half, devices, cols, takes, bloc...  30.5 us
    pallas_call x1, Pallas kernels, body(): pl.pallas_call(functools.partial(finish_kernel, half, blocks, halo, sweep...  3.09 us

profile of v7, /device:TPU:23, one launch (start us, length us, event | category | flops | bytes accessed | tf_op | source)
XLA Modules:
  0.0 34.2 jit_solution(18114679206952753830)
XLA Ops:
  0.6 30.5 %shard_map.41 = (f32[4,5,8,128]{3,2,1,0:T(8,128)}, f32[4,8,128]{2,1,0:T(8,128)}, f32[4,8,128]{2,1,0:T(8,128)}, f32[512,128]{1,0:T(8,128)}, f32[8,128]{1,0:T(8,128)}) custom-call(f32[64,384]{1,0:T(8,128)} %refs_0_.1, f32[384,128]{1,0:T(8,128)} %refs_1_.1), custom_call_target="tpu_custom_call" | custom-call | tf_op jit(solution)/shard_map/pallas_call | solution.py:520
  31.1 3.1 %shard_map.42 = (f32[64,384]{1,0:T(8,128)}, f32[384,128]{1,0:T(8,128)}) custom-call(f32[64,384]{1,0:T(8,128)} %refs_0_.1, f32[384,128]{1,0:T(8,128)} %refs_1_.1, f32[4,5,8,128]{3,2,1,0:T(8,128)} %get-tuple-element.7.refs_2_, f32[4,8,128]{2,1,0:T(8,128)} %get-tuple-element.8.refs_3_, f32[4,8,128]{2,1,0:T(8,128)} %get-tuple-element.9.refs_4_, ...), custom_call_target="tpu_custom_call" | custom-call | tf_op jit(solution)/shard_map/pallas_call | solution.py:536

commit v8 on v7

--- a/solution.py
+++ b/solution.py
@@ -141,14 +141,11 @@
         @pl.when(c == p)
         def _():
             for m in range(parts):
-                for to in reversed(range(cols)):
+                for to in range(cols):
                     if to != p:
                         along(p, m, to).start()
                 own(p, m).start()
                 spread(m, p, source(p, m))
-
-    for copy in halos:
-        copy.start()
 
     for m in range(parts):
         for p in reversed(range(pieces)):
@@ -347,6 +344,8 @@
     states = ()
     for s in range(last):
         states = phase(LAG * s, LAG * (s + 1), range(s + 1), states + (begin(s),))
+    for copy in halos:
+        copy.start()
     states = phase(LAG * last, steps, range(sweeps), states + (begin(last),))
     for s in range(1, sweeps):
         drain(s - 1, states[0])

time: 34.4 us -> 33.9 us (0.985)
  the two profiles are of different devices: /device:TPU:23 before, /device:TPU:29 now
where the time goes in v8:
time: 33.9 us; the launch traced here: 33.7 us
  Pallas kernels  33.1 us (98%)
  between operations  0.64 us (2%)
    pallas_call x1, Pallas kernels, body(): pl.pallas_call(functools.partial(kernel, half, devices, cols, takes, bloc...  30 us
    pallas_call x1, Pallas kernels, body(): pl.pallas_call(functools.partial(finish_kernel, half, blocks, halo, sweep...  3.1 us

profile of v8, /device:TPU:29, one launch (start us, length us, event | category | flops | bytes accessed | tf_op | source)
XLA Modules:
  0.0 33.7 jit_solution(16703095894389957784)
XLA Ops:
  0.6 30.0 %shard_map.41 = (f32[4,5,8,128]{3,2,1,0:T(8,128)}, f32[4,8,128]{2,1,0:T(8,128)}, f32[4,8,128]{2,1,0:T(8,128)}, f32[512,128]{1,0:T(8,128)}, f32[8,128]{1,0:T(8,128)}) custom-call(f32[64,384]{1,0:T(8,128)} %refs_0_.1, f32[384,128]{1,0:T(8,128)} %refs_1_.1), custom_call_target="tpu_custom_call" | custom-call | tf_op jit(solution)/shard_map/pallas_call | solution.py:519
  30.6 3.1 %shard_map.42 = (f32[64,384]{1,0:T(8,128)}, f32[384,128]{1,0:T(8,128)}) custom-call(f32[64,384]{1,0:T(8,128)} %refs_0_.1, f32[384,128]{1,0:T(8,128)} %refs_1_.1, f32[4,5,8,128]{3,2,1,0:T(8,128)} %get-tuple-element.7.refs_2_, f32[4,8,128]{2,1,0:T(8,128)} %get-tuple-element.8.refs_3_, f32[4,8,128]{2,1,0:T(8,128)} %get-tuple-element.9.refs_4_, ...), custom_call_target="tpu_custom_call" | custom-call | tf_op jit(solution)/shard_map/pallas_call | solution.py:535

commit v9 on v8

--- a/solution.py
+++ b/solution.py
@@ -9,7 +9,7 @@
 
 SWEEPS = 4
 LAG = 3
-AHEAD = 4
+AHEAD = 3
 EARLY = 3
 GROUP = 3
 

time: 33.9 us -> 33.4 us (0.985)
  the two profiles are of different devices: /device:TPU:29 before, /device:TPU:25 now
where the time goes in v9:
time: 33.4 us; the launch traced here: 33.2 us
  Pallas kernels  32.6 us (98%)
  between operations  0.64 us (2%)
    pallas_call x1, Pallas kernels, body(): pl.pallas_call(functools.partial(kernel, half, devices, cols, takes, bloc...  29.5 us
    pallas_call x1, Pallas kernels, body(): pl.pallas_call(functools.partial(finish_kernel, half, blocks, halo, sweep...  3.09 us

profile of v9, /device:TPU:25, one launch (start us, length us, event | category | flops | bytes accessed | tf_op | source)
XLA Modules:
  0.0 33.2 jit_solution(1379638822218069794)
XLA Ops:
  0.6 29.5 %shard_map.41 = (f32[4,5,8,128]{3,2,1,0:T(8,128)}, f32[4,8,128]{2,1,0:T(8,128)}, f32[4,8,128]{2,1,0:T(8,128)}, f32[512,128]{1,0:T(8,128)}, f32[8,128]{1,0:T(8,128)}) custom-call(f32[64,384]{1,0:T(8,128)} %refs_0_.1, f32[384,128]{1,0:T(8,128)} %refs_1_.1), custom_call_target="tpu_custom_call" | custom-call | tf_op jit(solution)/shard_map/pallas_call | solution.py:519
  30.1 3.1 %shard_map.42 = (f32[64,384]{1,0:T(8,128)}, f32[384,128]{1,0:T(8,128)}) custom-call(f32[64,384]{1,0:T(8,128)} %refs_0_.1, f32[384,128]{1,0:T(8,128)} %refs_1_.1, f32[4,5,8,128]{3,2,1,0:T(8,128)} %get-tuple-element.7.refs_2_, f32[4,8,128]{2,1,0:T(8,128)} %get-tuple-element.8.refs_3_, f32[4,8,128]{2,1,0:T(8,128)} %get-tuple-element.9.refs_4_, ...), custom_call_target="tpu_custom_call" | custom-call | tf_op jit(solution)/shard_map/pallas_call | solution.py:535

commit v10 on v9

--- a/solution.py
+++ b/solution.py
@@ -10,7 +10,7 @@
 SWEEPS = 4
 LAG = 3
 AHEAD = 3
-EARLY = 3
+EARLY = 4
 GROUP = 3
 
 

time: 33.4 us -> 33.4 us (level)
  no operation moved by 1% of the time
where the time goes in v10:
time: 33.4 us; the launch traced here: 33.2 us
  Pallas kernels  32.6 us (98%)
  between operations  0.64 us (2%)
    pallas_call x1, Pallas kernels, body(): pl.pallas_call(functools.partial(kernel, half, devices, cols, takes, bloc...  29.5 us
    pallas_call x1, Pallas kernels, body(): pl.pallas_call(functools.partial(finish_kernel, half, blocks, halo, sweep...  3.1 us

profile of v10, /device:TPU:25, one launch (start us, length us, event | category | flops | bytes accessed | tf_op | source)
XLA Modules:
  0.0 33.2 jit_solution(16742070754459415838)
XLA Ops:
  0.6 29.5 %shard_map.41 = (f32[4,5,8,128]{3,2,1,0:T(8,128)}, f32[4,8,128]{2,1,0:T(8,128)}, f32[4,8,128]{2,1,0:T(8,128)}, f32[512,128]{1,0:T(8,128)}, f32[8,128]{1,0:T(8,128)}) custom-call(f32[64,384]{1,0:T(8,128)} %refs_0_.1, f32[384,128]{1,0:T(8,128)} %refs_1_.1), custom_call_target="tpu_custom_call" | custom-call | tf_op jit(solution)/shard_map/pallas_call | solution.py:519
  30.1 3.1 %shard_map.42 = (f32[64,384]{1,0:T(8,128)}, f32[384,128]{1,0:T(8,128)}) custom-call(f32[64,384]{1,0:T(8,128)} %refs_0_.1, f32[384,128]{1,0:T(8,128)} %refs_1_.1, f32[4,5,8,128]{3,2,1,0:T(8,128)} %get-tuple-element.7.refs_2_, f32[4,8,128]{2,1,0:T(8,128)} %get-tuple-element.8.refs_3_, f32[4,8,128]{2,1,0:T(8,128)} %get-tuple-element.9.refs_4_, ...), custom_call_target="tpu_custom_call" | custom-call | tf_op jit(solution)/shard_map/pallas_call | solution.py:535
